TPU v7x, 256 devices: a whole 4x4x8 slice. The times are simulated.
256 devices in a mesh: tile: 32 (over z_lo, y, core), lev: 8 (over x, z_hi).
Axes of the slice: x: 4, y: 4, z: 8 (z_hi: 2, z_lo: 4; z = z_hi * 4 + z_lo), core: 2. Of those that a mesh axis runs over, the one named last changes fastest.
Arguments:
- costate_ending_fields: float32 [4, 16, 32, 32, 128], P(None, 'lev', 'tile'), may hold values from -6 to 6
- costate_ending_elevation: float32 [32, 32, 128], P('tile'), may hold values from -6 to 6
- upstream_transport_coefficient: float32 [16, 32, 32, 128], P('lev', 'tile'), may hold values from 0.05 to 0.45
- eastward_spread_coefficient: float32 [32, 32, 128], P('tile'), may hold values from 0.02 to 0.2
- interface_blending_coefficient: float32 [16, 32, 32, 128], P('lev', 'tile'), may hold values from 0.02 to 0.3
- thickness_sensitivity: float32 [4, 16, 32, 32, 128], P(None, 'lev', 'tile'), may hold values from -1.75 to 1.75
- layer_velocity_factor: float32 [16, 32, 32, 128], P('lev', 'tile'), may hold values from 0.02 to 0.1
- western_join_turned: int32 [32], replicated, may hold values from 0 to 1
- predicted_thermal_skin: float32 [32, 32, 128], P('tile'), may hold values from -6 to 6
- predicted_elevation: float32 [32, 32, 128], P('tile'), may hold values from -6 to 6
- measured_quantity: float32 [8, 32, 32, 512], P('lev', 'tile'), may hold values from -6 to 6
- measurement_precision: float32 [8, 32, 32, 512], P('lev', 'tile'), may hold values from 0.05 to 0.3
- measurement_sort: int32 [8, 32, 32, 512], P('lev', 'tile'), may hold values from 0 to 1
- sampled_location: int32 [8, 32, 32, 512], P('lev', 'tile'), may hold values from 0 to 4095
- active_entry_numbers: int32 [8, 32, 32], P('lev', 'tile'), may hold values from 0 to 512, as said below
Outputs:
- adj_state_start: float32 [4, 16, 32, 32, 128], P(None, 'lev', 'tile')
- adj_height_start: float32 [32, 32, 128], P('tile')
Inputs may be any that keep to these rules, and one draw needn't show every extreme that they name: `western_join_turned`: 1 means a rotated seam. `active_entry_numbers`: slots at or above the count carry no record; in every draw some destination tile has all 512 slots live from every source tile in every level group.
All inputs are finite; a program needn't handle non-finite values.
Results may differ from a plain program's by a relative error of at most 0.0003.
Values sent between devices are 32-bit elements; how exact they have to be, the bound alone decides.
No kernel may reach another device: no remote copies, remote signals or barrier semaphores. Data moves between devices by JAX's collectives and lax.ppermute only.
A program may use at most 64 MiB of HBM per device.

v0:
```python
import jax
import jax.numpy as jnp
from jax import lax
from jax.sharding import PartitionSpec as P

OUT_SIGN = (1.0, 1.0, -1.0, 1.0)
SEAM_ORDER = (0, 1, 3, 2)


def shifted(value, axis, steps):
    count = lax.axis_size(axis)
    pairs = [(source, (source + steps) % count) for source in range(count)]
    return lax.ppermute(value, axis, pairs)


def from_behind(block, axis, distance):
    devices = range(lax.axis_size(axis))
    route = [(i - distance, i) for i in devices if i - distance in devices]
    return lax.ppermute(block, axis, route)


def adjoint_step(lam_state, lam_height, flow_l, diff_l, mix_l, stretch_l, weight_l, rotated):
    scaled = flow_l[None] * lam_state
    advect = jnp.concatenate([scaled[..., 1:], jnp.zeros_like(scaled[..., :1])], axis=-1) - scaled
    edge = scaled[..., 0]
    sign = jnp.array(OUT_SIGN, jnp.float32)[:, None, None]
    order = jnp.array(SEAM_ORDER, jnp.int32)
    outgoing = jnp.where(rotated, sign * edge[order][..., ::-1], edge)
    incoming = shifted(outgoing, "tile", -1)
    advect = advect.at[..., -1].add(incoming)
    next_row = jnp.concatenate(
        [lam_state[..., 1:, :], jnp.zeros_like(lam_state[..., :1, :])], axis=-2
    )
    face_y = diff_l[None, None] * (next_row - lam_state)
    mix_row = face_y - jnp.concatenate(
        [jnp.zeros_like(face_y[..., :1, :]), face_y[..., :-1, :]], axis=-2
    )
    below = from_behind(lam_state[:, :1], "lev", -1)
    lower = jnp.concatenate([lam_state[:, 1:], below], axis=1)
    face_z = mix_l[None] * (lower - lam_state)
    above = from_behind(face_z[:, -1:], "lev", 1)
    mix_col = face_z - jnp.concatenate([above, face_z[:, :-1]], axis=1)
    new_state = lam_state + advect + mix_row + mix_col
    new_state = new_state.at[2].add(weight_l * lam_height[None])
    column_part = jnp.sum(stretch_l * lam_state, axis=(0, 1))
    new_height = lam_height + lax.psum(column_part, "lev")
    return (new_state, new_height)


def per_device(
    costate_ending_fields,
    costate_ending_elevation,
    upstream_transport_coefficient,
    eastward_spread_coefficient,
    interface_blending_coefficient,
    thickness_sensitivity,
    layer_velocity_factor,
    western_join_turned,
    predicted_thermal_skin,
    predicted_elevation,
    measured_quantity,
    measurement_precision,
    measurement_sort,
    sampled_location,
    active_entry_numbers,
):
    lev_dev = costate_ending_fields.shape[1]
    rows = costate_ending_fields.shape[3]
    cols = costate_ending_fields.shape[4]
    slots = measured_quantity.shape[3]
    lev_index = lax.axis_index("lev")
    tile_index = lax.axis_index("tile")
    level_total = lev_dev * lax.axis_size("lev")
    global_level = lev_index * lev_dev + jnp.arange(lev_dev, dtype=jnp.int32)
    mix_l = (
        interface_blending_coefficient[:, 0]
        * (global_level < level_total - 1).astype(jnp.float32)[:, None, None]
    )
    row_mask = (jnp.arange(rows) < rows - 1).astype(jnp.float32)[:, None]
    diff_l = eastward_spread_coefficient[0] * row_mask
    flow_l = upstream_transport_coefficient[:, 0]
    stretch_l = thickness_sensitivity[:, :, 0]
    weight_l = layer_velocity_factor[:, 0]
    rotated = western_join_turned[tile_index] == 1
    live = jnp.arange(slots, dtype=jnp.int32)[None, :] < active_entry_numbers[0, 0][:, None]
    packet = jnp.stack(
        [
            measured_quantity[0, 0],
            jnp.where(live, measurement_precision[0, 0], 0.0),
            measurement_sort[0, 0].astype(jnp.float32),
            sampled_location[0, 0].astype(jnp.float32),
        ]
    )
    arrived = lax.all_to_all(packet, "tile", split_axis=1, concat_axis=1, tiled=True)
    record_kind = arrived[2].astype(jnp.int32)
    mesh_point = arrived[3].astype(jnp.int32)
    marine_dynamics = jnp.where(
        record_kind == 0,
        predicted_thermal_skin.reshape(-1)[mesh_point],
        predicted_elevation.reshape(-1)[mesh_point],
    )
    misfit = arrived[1] * (marine_dynamics - arrived[0])
    target = (record_kind * (rows * cols) + mesh_point).reshape(-1)
    maps = (
        jnp.zeros((2 * rows * cols,), jnp.float32)
        .at[target]
        .add(misfit.reshape(-1))
        .reshape(2, rows, cols)
    )
    maps = lax.psum(maps, "lev")
    lam_state = costate_ending_fields[:, :, 0]
    lam_state = lam_state.at[0, 0].add(jnp.where(lev_index == 0, maps[0], 0.0))
    lam_height = costate_ending_elevation[0] + maps[1]
    for turn in range(2):
        lam_state, lam_height = adjoint_step(
            lam_state, lam_height, flow_l, diff_l, mix_l, stretch_l, weight_l, rotated
        )
    return (lam_state[:, :, None], lam_height[None])


def solution(mesh):
    placed = (
        P(None, "lev", "tile", None, None),
        P("tile", None, None),
        P("lev", "tile", None, None),
        P("tile", None, None),
        P("lev", "tile", None, None),
        P(None, "lev", "tile", None, None),
        P("lev", "tile", None, None),
        P(),
        P("tile", None, None),
        P("tile", None, None),
        P("lev", "tile", None, None),
        P("lev", "tile", None, None),
        P("lev", "tile", None, None),
        P("lev", "tile", None, None),
        P("lev", "tile", None),
    )
    return jax.shard_map(
        per_device,
        mesh=mesh,
        in_specs=placed,
        out_specs=(P(None, "lev", "tile", None, None), P("tile", None, None)),
        check_vma=False,
    )
```

profile of v0, /device:TPU:38, one launch (start us, length us, event | category | flops | bytes accessed | tf_op | source)
XLA Modules:
  0.0 480.6 jit_solution(5255978705896090962)
XLA Ops:
  0.7 0.9 stack_squeeze.3
  1.6 0.8 copy-done.13
  2.5 0.8 copy-done.14
  3.5 1.0 pad_maximum_fusion
  4.5 8.9 %all-to-all-start = ((f32[4,32,512]{2,0,1:T(4,128)}), f32[4,32,512]{2,0,1:T(4,128)S(1)}, u32[]{:S(2)}, u32[]{:S(2)}) async-start(f32[4,32,512]{2,0,1:T(4,128)} %pad_maximum_fusion), calls=%async_computation | async-start | bytes 524288 | tf_op jit(solution)/shard_map/all_to_all | solution.py:94
  14.8 0.6 copy-done.17
  16.4 0.6 copy-done.16
  17.2 0.6 copy-done.23
  19.1 4.3 all-to-all-done
  23.9 90.5 %gather_fusion.1 = f32[16384]{0:T(1024)S(1)} fusion(f32[4096]{0:T(1024)S(1)} %bitcast.73, s32[16384]{0:T(1024)S(1)} %broadcast_clamp_fusion), kind=kCustom, calls=%fused_computation.1 | custom fusion | bytes 196608 | tf_op jit(solution)/shard_map/gather | solution.py:100
  114.5 90.5 %gather_fusion = f32[16384]{0:T(1024)S(1)} fusion(f32[4096]{0:T(1024)S(1)} %bitcast.74, s32[16384]{0:T(1024)S(1)} %broadcast_clamp_fusion), kind=kCustom, calls=%fused_computation | custom fusion | bytes 196608 | tf_op jit(solution)/shard_map/gather | solution.py:99
  205.4 85.8 %scatter_custom_fusion = f32[8192]{0:T(1024)S(1)} fusion(s32[16384]{0:T(1024)S(1)} %bitcast.86, f32[16384]{0:T(1024)S(1)} %subtract_multiply_fusion.2, f32[]{:T(128)} %constant.154.clone.1), kind=kCustom, calls=%fused_computation.50 | custom fusion | flops 16384 | bytes 32772 | tf_op jit(solution)/shard_map/scatter-add | solution.py:107
  291.4 54.0 %psum.21 = f32[2,32,128]{1,2,0:T(8,128)S(1)} all-reduce(f32[2,32,128]{1,2,0:T(8,128)S(1)} %copy.109), channel_id=1, replica_groups=mesh['tile'=32,'lev'=8] {'lev'}, use_global_device_ids=true, to_apply=%region_1.2 | all-reduce | flops 8192 | bytes 65536 | tf_op jit(solution)/shard_map/psum | solution.py:110
  345.4 1.6 scatter-add.25
  347.5 1.9 collective-permute-start.1
  350.0 12.1 %collective-permute-done.1 = f32[4,1,32,128]{2,1,0,3:T(1,128)S(1)} collective-permute-done((f32[4,1,32,128]{2,1,0,3:T(1,128)S(1)}, f32[4,1,32,128]{2,1,0,3:T(1,128)S(1)}, u32[]{:S(2)}, u32[]{:S(2)}) %collective-permute-start.1) | collective-permute-done | bytes 65568 | tf_op jit(solution)/shard_map/ppermute | solution.py:19
  362.1 1.2 broadcast_multiply_fusion.1
  364.1 0.7 copy-done.20
  365.6 1.9 collective-permute-start.2
  367.5 17.1 %collective-permute-done.2 = f32[4,1,32,128]{2,1,0,3:T(1,128)S(1)} collective-permute-done((f32[4,1,32,128]{2,1,0,3:T(1,128)S(1)}, f32[4,1,32,128]{2,1,0,3:T(1,128)S(1)}, u32[]{:S(2)}, u32[]{:S(2)}) %collective-permute-start.2) | collective-permute-done | bytes 65568 | tf_op jit(solution)/shard_map/ppermute | solution.py:19
  384.7 1.2 fusion.1
  386.0 1.1 fusion.17
  387.1 2.6 collective-permute-start.4
  390.7 16.0 %collective-permute-done.4 = f32[4,1,32,128]{2,1,0,3:T(1,128)S(1)} collective-permute-done((f32[4,1,32,128]{2,1,0,3:T(1,128)S(1)}, f32[4,1,32,128]{2,1,0,3:T(1,128)S(1)}, u32[]{:S(2)}, u32[]{:S(2)}) %collective-permute-start.4) | collective-permute-done | bytes 65568 | tf_op jit(solution)/shard_map/ppermute | solution.py:19
  406.7 0.7 copy-done.9
  407.4 3.7 fusion.5
  413.1 48.6 %all-reduce.6 = (f32[32,128]{0,1:T(8,128)S(1)}, f32[32,128]{0,1:T(8,128)S(1)}) all-reduce(f32[32,128]{0,1:T(8,128)S(1)} %copy-done.8, f32[32,128]{0,1:T(8,128)S(1)} %copy-done.7), channel_id=1, replica_groups=mesh['tile'=32,'lev'=8] {'lev'}, use_global_device_ids=true, to_apply=%region_3.4 | all-reduce | flops 8192 | bytes 65536 | tf_op jit(solution)/shard_map/psum | solution.py:46
  461.8 0.7 copy.119
  462.5 7.3 %collective-permute-start.5 = (f32[4,1,32,128]{2,1,0,3:T(1,128)S(1)}, f32[4,1,32,128]{2,1,0,3:T(1,128)S(1)}, u32[]{:S(2)}, u32[]{:S(2)}) collective-permute-start(f32[4,1,32,128]{2,1,0,3:T(1,128)S(1)} %get-tuple-element.81), channel_id=1, source_target_pairs={{0,1},{1,2},{2,3},{3,4},{4,5},{5,6},{6,7},{8,9},{9,10},{10,11},{11... | collective-permute-start | bytes 196616 | tf_op jit(solution)/shard_map/ppermute | solution.py:19
  469.9 8.4 %collective-permute-done.5 = f32[4,1,32,128]{2,1,0,3:T(1,128)S(1)} collective-permute-done((f32[4,1,32,128]{2,1,0,3:T(1,128)S(1)}, f32[4,1,32,128]{2,1,0,3:T(1,128)S(1)}, u32[]{:S(2)}, u32[]{:S(2)}) %collective-permute-start.5) | collective-permute-done | bytes 65568 | tf_op jit(solution)/shard_map/ppermute | solution.py:19
  478.2 1.2 fusion.3
  479.6 1.0 copy.118
  (98 shorter events, 10.1 us)
Async XLA Ops:
  0.6 23.3 %copy-start = (f32[1,32,128]{2,1,0:T(8,128)S(1)}, f32[1,32,128]{2,1,0:T(8,128)}, u32[]{:S(2)}) copy-start(f32[1,32,128]{2,1,0:T(8,128)} %param.38) | copy-start | bytes 49156
  0.6 0.9 copy-start.12
  1.6 0.8 copy-start.13
  2.4 0.8 copy-start.14
  2.4 0.8 copy-start.21
  4.5 9.0 %copy-start.19 = (f32[1,32,128]{2,1,0:T(8,128)S(1)}, f32[1,32,128]{2,1,0:T(8,128)}, u32[]{:S(2)}) copy-start(f32[1,32,128]{2,1,0:T(8,128)} %param.32) | copy-start | bytes 49156
  4.5 9.0 %copy-start.10 = (f32[4,2,1,32,128]{4,3,2,1,0:T(8,128)S(1)}, f32[4,2,1,32,128]{4,3,2,1,0:T(8,128)}, u32[]{:S(2)}) copy-start(f32[4,2,1,32,128]{4,3,2,1,0:T(8,128)} %param.29) | copy-start | bytes 393220
  4.5 19.0 %all-to-all-start = ((f32[4,32,512]{2,0,1:T(4,128)}), f32[4,32,512]{2,0,1:T(4,128)S(1)}, u32[]{:S(2)}, u32[]{:S(2)}) async-start(f32[4,32,512]{2,0,1:T(4,128)} %pad_maximum_fusion), calls=%async_computation | async-start | bytes 524288 | tf_op jit(solution)/shard_map/all_to_all | solution.py:94
  14.0 0.7 copy-start.18
  14.7 0.8 copy-start.17
  15.6 0.8 copy-start.15
  16.3 0.8 copy-start.16
  17.1 345.1 %copy-start.2 = (f32[2,32,128]{1,0,2:T(2,128)}, f32[2,32,128]{1,0,2:T(2,128)S(1)}, u32[]{:S(2)}) copy-start(f32[2,32,128]{1,0,2:T(2,128)S(1)} %copy.111) | copy-start | bytes 98308
  17.2 0.7 copy-start.23
  18.4 0.7 copy-start.22
  23.9 90.6 %copy-start.1 = (f32[1,32,128]{2,1,0:T(8,128)S(1)}, f32[1,32,128]{2,1,0:T(8,128)}, u32[]{:S(2)}) copy-start(f32[1,32,128]{2,1,0:T(8,128)} %param.37) | copy-start | bytes 49156
  347.5 14.7 %collective-permute-start.1 = (f32[4,1,32,128]{2,1,0,3:T(1,128)S(1)}, f32[4,1,32,128]{2,1,0,3:T(1,128)S(1)}, u32[]{:S(2)}, u32[]{:S(2)}) collective-permute-start(f32[4,1,32,128]{2,1,0,3:T(1,128)S(1)} %get-tuple-element.91), channel_id=1, source_target_pairs={{1,0},{2,1},{3,2},{4,3},{5,4},{6,5},{7,6},{9,8},{10,9},{11,10},{12... | collective-permute-start | bytes 196616 | tf_op jit(solution)/shard_map/ppermute | solution.py:19
  349.4 36.4 %copy-start.5 = (f32[32,128]{0,1:T(8,128)}, f32[32,128]{0,1:T(8,128)S(1)}, u32[]{:S(2)}) copy-start(f32[32,128]{0,1:T(8,128)S(1)} %fusion.9) | copy-start | bytes 49156
  364.1 0.7 copy-start.20
  364.8 2.7 collective-permute-start
  365.6 19.1 %collective-permute-start.2 = (f32[4,1,32,128]{2,1,0,3:T(1,128)S(1)}, f32[4,1,32,128]{2,1,0,3:T(1,128)S(1)}, u32[]{:S(2)}, u32[]{:S(2)}) collective-permute-start(f32[4,1,32,128]{2,1,0,3:T(1,128)S(1)} %get-tuple-element.88), channel_id=1, source_target_pairs={{0,1},{1,2},{2,3},{3,4},{4,5},{5,6},{6,7},{8,9},{9,10},{10,11},{11... | collective-permute-start | bytes 196616 | tf_op jit(solution)/shard_map/ppermute | solution.py:19
  386.0 3.7 copy-start.11
  387.1 19.6 %collective-permute-start.4 = (f32[4,1,32,128]{2,1,0,3:T(1,128)S(1)}, f32[4,1,32,128]{2,1,0,3:T(1,128)S(1)}, u32[]{:S(2)}, u32[]{:S(2)}) collective-permute-start(f32[4,1,32,128]{2,1,0,3:T(1,128)S(1)} %get-tuple-element.84), channel_id=1, source_target_pairs={{1,0},{2,1},{3,2},{4,3},{5,4},{6,5},{7,6},{9,8},{10,9},{11,10},{12... | collective-permute-start | bytes 196616 | tf_op jit(solution)/shard_map/ppermute | solution.py:19
  390.1 17.3 %copy-start.3 = (f32[2,32,128]{1,0,2:T(2,128)S(1)}, f32[2,32,128]{1,0,2:T(2,128)}, u32[]{:S(2)}) copy-start(f32[2,32,128]{1,0,2:T(2,128)} %copy-done.2) | copy-start | bytes 98308
  390.1 17.3 %copy-start.4 = (f32[4,1,32,128]{2,1,0,3:T(1,128)S(1)}, f32[4,1,32,128]{2,1,0,3:T(1,128)}, u32[]{:S(2)}) copy-start(f32[4,1,32,128]{2,1,0,3:T(1,128)} %get-tuple-element.83) | copy-start | bytes 196612
  406.7 0.7 copy-start.9
  411.9 58.0 %collective-permute-start.3 = (f32[4,2,32]{2,1,0:T(2,128)S(1)}, f32[4,2,32]{2,1,0:T(2,128)S(1)}, u32[]{:S(2)}, u32[]{:S(2)}) collective-permute-start(f32[4,2,32]{2,1,0:T(2,128)S(1)} %multiply_select_fusion), channel_id=1, source_target_pairs={{0,248},{8,0},{16,8},{24,16},{32,24},{40,32},{48,40},{56,48},{64,5... | collective-permute-start | bytes 3080 | tf_op jit(solution)/shard_map/ppermute | solution.py:13
  412.3 0.8 copy-start.7
  412.3 0.9 copy-start.8
  413.1 48.7 %copy-start.6 = (f32[32,128]{0,1:T(8,128)S(1)}, f32[32,128]{0,1:T(8,128)}, u32[]{:S(2)}) copy-start(f32[32,128]{0,1:T(8,128)} %copy-done.5) | copy-start | bytes 49156
  462.5 15.7 %collective-permute-start.5 = (f32[4,1,32,128]{2,1,0,3:T(1,128)S(1)}, f32[4,1,32,128]{2,1,0,3:T(1,128)S(1)}, u32[]{:S(2)}, u32[]{:S(2)}) collective-permute-start(f32[4,1,32,128]{2,1,0,3:T(1,128)S(1)} %get-tuple-element.81), channel_id=1, source_target_pairs={{0,1},{1,2},{2,3},{3,4},{4,5},{5,6},{6,7},{8,9},{9,10},{10,11},{11... | collective-permute-start | bytes 196616 | tf_op jit(solution)/shard_map/ppermute | solution.py:19
where the time goes:
time: 481 us
  local copies, waits for them, and re-layouts  199 us (41%)
  blocking collectives  103 us (21%)
  other arithmetic  96.2 us (20%)
  waiting for transfers between devices  57.9 us (12%)
  starting transfers between devices  22.7 us (5%)
    gather x1, local copies, waits for them, and re-layouts, per_device(): predicted_elevation.reshape(-1)[mesh_point]  90.5 us
    gather x1, local copies, waits for them, and re-layouts, per_device(): predicted_thermal_skin.reshape(-1)[mesh_point]  90.5 us
    scatter-add x1, other arithmetic, per_device(): maps = jnp.zeros((2 * rows * cols,), jnp.float32).at[target].add(misfit.r...  85.8 us
    psum x1, blocking collectives, per_device(): maps = lax.psum(maps, 'lev')  54 us
    ppermute x4, waiting for transfers between devices, from_behind(): return lax.ppermute(block, axis, route)  53.6 us
    psum x1, blocking collectives, adjoint_step(): new_height = lam_height + lax.psum(column_part, 'lev')  48.6 us
    ppermute x4, starting transfers between devices, from_behind(): return lax.ppermute(block, axis, route)  13.7 us
  transfers between devices with their start and end apart: 7, of which 5 were waited for; matrix products, arithmetic and copies ran while one was open for 1% of the time, Pallas kernels for 0%

commit v1 on v0

--- a/solution.py
+++ b/solution.py
@@ -1,6 +1,8 @@
 import jax
 import jax.numpy as jnp
 from jax import lax
+from jax.experimental import pallas as pl
+from jax.experimental.pallas import tpu as pltpu
 from jax.sharding import PartitionSpec as P
 
 OUT_SIGN = (1.0, 1.0, -1.0, 1.0)
@@ -17,6 +19,64 @@
     devices = range(lax.axis_size(axis))
     route = [(i - distance, i) for i in devices if i - distance in devices]
     return lax.ppermute(block, axis, route)
+
+
+PIECES = 3
+ROWS_AT_ONCE = 8
+
+
+def maps_kernel(records, thermal, elevation, out, total):
+    sources, slots = records.shape[1:]
+    rows, cols = thermal.shape
+    half = jnp.bfloat16
+    row_of = lax.broadcasted_iota(jnp.int32, (2 * rows, slots), 0).astype(jnp.float32).astype(half)
+    col_of = lax.broadcasted_iota(jnp.int32, (cols, slots), 0).astype(jnp.float32).astype(half)
+    nothing = jnp.zeros((2 * rows, slots), half)
+    one, zero = jnp.ones((cols, slots), half), jnp.zeros((cols, slots), half)
+    total[...] = jnp.zeros_like(total)
+
+    def body(i, carry):
+        left, right = [], []
+        for j in range(ROWS_AT_ONCE):
+            weight, scaled, kind, place = (records[n, pl.ds(i * ROWS_AT_ONCE + j, 1), :] for n in range(4))
+            row = jnp.floor(place * (1.0 / cols))
+            col = place - row * cols
+            row = row + kind * rows
+            here = jnp.broadcast_to(row.astype(half), nothing.shape) == row_of
+            parts = []
+            for rest in (weight, scaled):
+                for _ in range(PIECES):
+                    piece = rest.astype(half)
+                    rest = rest - piece.astype(jnp.float32)
+                    parts.append(jnp.where(here, jnp.broadcast_to(piece, nothing.shape), nothing))
+            left.append(jnp.concatenate(parts, 0))
+            right.append(jnp.where(jnp.broadcast_to(col.astype(half), one.shape) == col_of, one, zero))
+        total[...] += lax.dot_general(
+            jnp.concatenate(left, 1),
+            jnp.concatenate(right, 1),
+            (((1,), (1,)), ((), ())),
+            preferred_element_type=jnp.float32,
+        )
+        return carry
+
+    lax.fori_loop(0, sources // ROWS_AT_ONCE, body, 0)
+    step = 2 * rows
+    weights = sum(total[n * step : (n + 1) * step] for n in range(PIECES))
+    values = sum(total[n * step : (n + 1) * step] for n in range(PIECES, 2 * PIECES))
+    out[0] = thermal[...] * weights[:rows] - values[:rows]
+    out[1] = elevation[...] * weights[rows:] - values[rows:]
+
+
+def local_maps(records, thermal, elevation):
+    rows, cols = thermal.shape
+    return pl.pallas_call(
+        maps_kernel,
+        out_shape=jax.ShapeDtypeStruct((2, rows, cols), jnp.float32),
+        in_specs=[pl.BlockSpec(memory_space=pltpu.VMEM)] * 3,
+        out_specs=pl.BlockSpec(memory_space=pltpu.VMEM),
+        scratch_shapes=[pltpu.VMEM((4 * PIECES * rows, cols), jnp.float32)],
+        name="maps",
+    )(records, thermal, elevation)
 
 
 def adjoint_step(lam_state, lam_height, flow_l, diff_l, mix_l, stretch_l, weight_l, rotated):
@@ -83,30 +143,17 @@
     weight_l = layer_velocity_factor[:, 0]
     rotated = western_join_turned[tile_index] == 1
     live = jnp.arange(slots, dtype=jnp.int32)[None, :] < active_entry_numbers[0, 0][:, None]
+    weight = jnp.where(live, measurement_precision[0, 0], 0.0)
     packet = jnp.stack(
         [
-            measured_quantity[0, 0],
-            jnp.where(live, measurement_precision[0, 0], 0.0),
+            weight,
+            weight * measured_quantity[0, 0],
             measurement_sort[0, 0].astype(jnp.float32),
             sampled_location[0, 0].astype(jnp.float32),
         ]
     )
     arrived = lax.all_to_all(packet, "tile", split_axis=1, concat_axis=1, tiled=True)
-    record_kind = arrived[2].astype(jnp.int32)
-    mesh_point = arrived[3].astype(jnp.int32)
-    marine_dynamics = jnp.where(
-        record_kind == 0,
-        predicted_thermal_skin.reshape(-1)[mesh_point],
-        predicted_elevation.reshape(-1)[mesh_point],
-    )
-    misfit = arrived[1] * (marine_dynamics - arrived[0])
-    target = (record_kind * (rows * cols) + mesh_point).reshape(-1)
-    maps = (
-        jnp.zeros((2 * rows * cols,), jnp.float32)
-        .at[target]
-        .add(misfit.reshape(-1))
-        .reshape(2, rows, cols)
-    )
+    maps = local_maps(arrived, predicted_thermal_skin[0], predicted_elevation[0])
     maps = lax.psum(maps, "lev")
     lam_state = costate_ending_fields[:, :, 0]
     lam_state = lam_state.at[0, 0].add(jnp.where(lev_index == 0, maps[0], 0.0))

time: 481 us -> 220 us (0.46)
  local copies, waits for them, and re-layouts: 199 us -> 19.8 us
  other arithmetic: 96.2 us -> 13.3 us
  blocking collectives: 103 us -> 97 us
  Pallas kernels: 0 us -> 5.62 us
    gather x2 -> x0, local copies, waits for them, and re-layouts: 181 us -> none  [the longest x1 90.5 us: per_device(): predicted_elevation.reshape(-1)[mesh_point]]
    scatter-add x1 -> x0, other arithmetic: 85.8 us -> none  [per_device(): maps = jnp.zeros((2 * rows * cols,), jnp.float32).at[target].add(misfit.r...]
    pallas_call x0 -> x1, Pallas kernels: none -> 5.62 us  [local_maps(): pl.pallas_call(maps_kernel, out_shape=jax.ShapeDtypeStruct((2, rows, cols...]
  transfers between devices with their start and end apart: 7 -> 7, of which waited for: 5 -> 5; matrix products, arithmetic and copies ran while one was open for 1% -> 3% of each run, Pallas kernels for 0% -> 0%
where the time goes in v1:
time: 220 us; the launch traced here: 217 us
  blocking collectives  97 us (44%)
  waiting for transfers between devices  59.9 us (27%)
  local copies, waits for them, and re-layouts  19.8 us (9%)
  starting transfers between devices  19.7 us (9%)
  other arithmetic  13.3 us (6%)
  Pallas kernels  5.62 us (3%)
    ppermute x4, waiting for transfers between devices, from_behind(): return lax.ppermute(block, axis, route)  55.4 us
    psum x1, blocking collectives, per_device(): maps = lax.psum(maps, 'lev')  50.4 us
    psum x1, blocking collectives, adjoint_step(): new_height = lam_height + lax.psum(column_part, 'lev')  46.6 us
    ppermute x4, starting transfers between devices, from_behind(): return lax.ppermute(block, axis, route)  10.8 us
    all_to_all x1, starting transfers between devices, per_device(): lax.all_to_all(packet, 'tile', split_axis=1, concat_axis=1, tiled=True)  8.93 us
    unnamed x55, local copies, waits for them, and re-layouts  8.91 us
    pallas_call x1, Pallas kernels, local_maps(): pl.pallas_call(maps_kernel, out_shape=jax.ShapeDtypeStruct((2, rows, cols...  5.62 us
    all_to_all x1, waiting for transfers between devices, per_device(): lax.all_to_all(packet, 'tile', split_axis=1, concat_axis=1, tiled=True)  4.54 us
  transfers between devices with their start and end apart: 7, of which 5 were waited for; matrix products, arithmetic and copies ran while one was open for 3% of the time, Pallas kernels for 0%

profile of v1, /device:TPU:38, one launch (start us, length us, event | category | flops | bytes accessed | tf_op | source)
XLA Modules:
  0.0 217.1 jit_solution(1897435677431301775)
XLA Ops:
  0.6 0.9 convert_element_type.46
  2.6 1.0 pad_maximum_fusion
  3.5 8.9 %all-to-all-start = ((f32[4,32,512]{2,0,1:T(4,128)}), f32[4,32,512]{2,0,1:T(4,128)S(1)}, u32[]{:S(2)}, u32[]{:S(2)}) async-start(f32[4,32,512]{2,0,1:T(4,128)} %pad_maximum_fusion), calls=%async_computation | async-start | bytes 524288 | tf_op jit(solution)/shard_map/all_to_all | solution.py:155
  18.0 4.5 %all-to-all-done = f32[4,32,512]{2,0,1:T(4,128)S(1)} async-done(((f32[4,32,512]{2,0,1:T(4,128)}), f32[4,32,512]{2,0,1:T(4,128)S(1)}, u32[]{:S(2)}, u32[]{:S(2)}) %all-to-all-start) | async-done | bytes 262176 | tf_op jit(solution)/shard_map/all_to_all | solution.py:155
  22.5 0.8 copy.71.records
  23.3 5.6 %maps.1 = f32[2,32,128]{2,1,0:T(8,128)} custom-call(f32[4,32,512]{2,1,0:T(8,128)} %copy.71.records, f32[32,128]{1,0:T(8,128)} %bitcast.66, f32[32,128]{1,0:T(8,128)} %bitcast.67), custom_call_target="tpu_custom_call" | custom-call | tf_op jit(solution)/shard_map/maps/pallas_call | solution.py:72
  28.9 50.4 %psum.21 = f32[2,32,128]{2,1,0:T(8,128)S(1)} all-reduce(f32[2,32,128]{2,1,0:T(8,128)} %maps.1), channel_id=1, replica_groups=mesh['tile'=32,'lev'=8] {'lev'}, use_global_device_ids=true, to_apply=%region_0.1 | all-reduce | flops 8192 | bytes 65536 | tf_op jit(solution)/shard_map/psum | solution.py:157
  79.4 1.6 scatter-add.16
  81.5 1.9 collective-permute-start.1
  84.0 0.7 copy.77
  84.8 11.4 %collective-permute-done.1 = f32[4,1,32,128]{2,1,0,3:T(1,128)S(1)} collective-permute-done((f32[4,1,32,128]{2,1,0,3:T(1,128)S(1)}, f32[4,1,32,128]{2,1,0,3:T(1,128)S(1)}, u32[]{:S(2)}, u32[]{:S(2)}) %collective-permute-start.1) | collective-permute-done | bytes 65568 | tf_op jit(solution)/shard_map/ppermute | solution.py:21
  96.1 0.7 copy-done.7
  96.8 2.2 %broadcast_multiply_fusion.1 = (f32[4,2,32,128]{2,1,0,3:T(2,128)S(1)}, f32[4,2,32,128]{2,1,0,3:T(2,128)S(1)}, f32[4,2,32,128]{2,1,0,3:T(2,128)S(1)}) fusion(f32[4,2,32,128]{2,1,0,3:T(2,128)S(1)} %scatter-add.16, f32[2,32,128]{1,0,2:T(2,128)S(1)} %copy.73, f32[4,1,32,128]{2,1,0,3:T(1,128)} %copy-done.7, f32[4,1,32,128]{2,1,0,3:T(1,128)S(1)} %get-tuple-element.88, ...), kind=kLoop, calls=%fused_computation.20 | loop fusion | flops 196608 | bytes 864256 | tf_op jit(solution)/shard_map/mul | solution.py:83
  99.1 0.7 gather_fusion
  101.4 1.9 collective-permute-start.2
  103.3 18.1 %collective-permute-done.2 = f32[4,1,32,128]{2,1,0,3:T(1,128)S(1)} collective-permute-done((f32[4,1,32,128]{2,1,0,3:T(1,128)S(1)}, f32[4,1,32,128]{2,1,0,3:T(1,128)S(1)}, u32[]{:S(2)}, u32[]{:S(2)}) %collective-permute-start.2) | collective-permute-done | bytes 65568 | tf_op jit(solution)/shard_map/ppermute | solution.py:21
  121.4 1.2 fusion.1
  122.7 1.1 fusion.15
  123.8 2.9 %collective-permute-start.4 = (f32[4,1,32,128]{2,1,0,3:T(1,128)S(1)}, f32[4,1,32,128]{2,1,0,3:T(1,128)S(1)}, u32[]{:S(2)}, u32[]{:S(2)}) collective-permute-start(f32[4,1,32,128]{2,1,0,3:T(1,128)S(1)} %get-tuple-element.82), channel_id=1, source_target_pairs={{1,0},{2,1},{3,2},{4,3},{5,4},{6,5},{7,6},{9,8},{10,9},{11,10},{12... | collective-permute-start | bytes 196616 | tf_op jit(solution)/shard_map/ppermute | solution.py:21
  127.8 15.3 %collective-permute-done.4 = f32[4,1,32,128]{2,1,0,3:T(1,128)S(1)} collective-permute-done((f32[4,1,32,128]{2,1,0,3:T(1,128)S(1)}, f32[4,1,32,128]{2,1,0,3:T(1,128)S(1)}, u32[]{:S(2)}, u32[]{:S(2)}) %collective-permute-start.4) | collective-permute-done | bytes 65568 | tf_op jit(solution)/shard_map/ppermute | solution.py:21
  143.1 0.7 copy-done.5
  143.8 3.7 %fusion.5 = (f32[32,128]{0,1:T(8,128)}, f32[32,128]{0,1:T(8,128)}, f32[4,2,32,128]{2,1,0,3:T(2,128)S(1)}, f32[4,2,32,128]{2,1,0,3:T(2,128)S(1)}, f32[4,2,32,128]{2,1,0,3:T(2,128)S(1)}) fusion(f32[4,2,32,128]{2,1,0,3:T(2,128)S(1)} %fusion.8, f32[4,2,1,32,128]{3,1,0,4,2:T(2,128)S(1)} %copy.78, f32[4,2,32,128]{2,1,0,3:T(2,128)S(1)} %scatter-add.16, ...), kind=kLoop, calls=%fused_computation.13 | loop fusion | flops 319488 | bytes 1159168 | tf_op jit(solution)/shard_map/reduce_sum | solution.py:105
  147.5 0.8 copy-done.4
  148.3 0.7 copy.82
  149.0 0.7 gather_fusion.1
  150.4 0.7 multiply_select_fusion
  151.0 0.7 copy.79
  152.8 46.6 %all-reduce.6 = (f32[32,128]{1,0:T(8,128)S(1)}, f32[32,128]{1,0:T(8,128)S(1)}) all-reduce(f32[32,128]{1,0:T(8,128)S(1)} %copy-done.11, f32[32,128]{1,0:T(8,128)S(1)} %copy-done.10), channel_id=1, replica_groups=mesh['tile'=32,'lev'=8] {'lev'}, use_global_device_ids=true, to_apply=%region_2.3 | all-reduce | flops 8192 | bytes 65536 | tf_op jit(solution)/shard_map/psum | solution.py:106
  200.1 4.0 %collective-permute-start.5 = (f32[4,1,32,128]{2,1,0,3:T(1,128)S(1)}, f32[4,1,32,128]{2,1,0,3:T(1,128)S(1)}, u32[]{:S(2)}, u32[]{:S(2)}) collective-permute-start(f32[4,1,32,128]{2,1,0,3:T(1,128)S(1)} %get-tuple-element.79), channel_id=1, source_target_pairs={{0,1},{1,2},{2,3},{3,4},{4,5},{5,6},{6,7},{8,9},{9,10},{10,11},{11... | collective-permute-start | bytes 196616 | tf_op jit(solution)/shard_map/ppermute | solution.py:21
  204.1 10.7 %collective-permute-done.5 = f32[4,1,32,128]{2,1,0,3:T(1,128)S(1)} collective-permute-done((f32[4,1,32,128]{2,1,0,3:T(1,128)S(1)}, f32[4,1,32,128]{2,1,0,3:T(1,128)S(1)}, u32[]{:S(2)}, u32[]{:S(2)}) %collective-permute-start.5) | collective-permute-done | bytes 65568 | tf_op jit(solution)/shard_map/ppermute | solution.py:21
  214.8 1.2 fusion.3
  216.1 1.0 copy.83
  (90 shorter events, 12.3 us)
Async XLA Ops:
  0.6 0.9 copy-start.12
  1.5 0.8 copy-start.13
  1.6 0.9 copy-start.14
  1.7 0.7 copy-start.22
  3.5 8.9 %copy-start.19 = (f32[1,32,128]{2,1,0:T(8,128)S(1)}, f32[1,32,128]{2,1,0:T(8,128)}, u32[]{:S(2)}) copy-start(f32[1,32,128]{2,1,0:T(8,128)} %param.32) | copy-start | bytes 49156
  3.5 19.0 %all-to-all-start = ((f32[4,32,512]{2,0,1:T(4,128)}), f32[4,32,512]{2,0,1:T(4,128)S(1)}, u32[]{:S(2)}, u32[]{:S(2)}) async-start(f32[4,32,512]{2,0,1:T(4,128)} %pad_maximum_fusion), calls=%async_computation | async-start | bytes 524288 | tf_op jit(solution)/shard_map/all_to_all | solution.py:155
  12.6 0.8 copy-start.17
  12.7 84.2 %copy-start.1 = (f32[32,128]{0,1:T(8,128)}, f32[32,128]{0,1:T(8,128)S(1)}, u32[]{:S(2)}) copy-start(f32[32,128]{0,1:T(8,128)S(1)} %copy.74) | copy-start | bytes 49156
  13.4 0.8 copy-start.15
  14.2 0.8 copy-start.16
  14.2 0.9 copy-start.8
  15.4 0.7 copy-start.24
  16.7 0.7 copy-start.23
  81.1 2.4 %copy-start.18 = (f32[1,32,128]{2,1,0:T(8,128)S(1)}, f32[1,32,128]{2,1,0:T(8,128)}, u32[]{:S(2)}) copy-start(f32[1,32,128]{2,1,0:T(8,128)} %param.30) | copy-start | bytes 49156
  81.5 14.6 %collective-permute-start.1 = (f32[4,1,32,128]{2,1,0,3:T(1,128)S(1)}, f32[4,1,32,128]{2,1,0,3:T(1,128)S(1)}, u32[]{:S(2)}, u32[]{:S(2)}) collective-permute-start(f32[4,1,32,128]{2,1,0,3:T(1,128)S(1)} %get-tuple-element.89), channel_id=1, source_target_pairs={{1,0},{2,1},{3,2},{4,3},{5,4},{6,5},{7,6},{9,8},{10,9},{11,10},{12... | collective-permute-start | bytes 196616 | tf_op jit(solution)/shard_map/ppermute | solution.py:21
  96.1 0.7 copy-start.7
  99.9 0.7 copy-start.20
  100.6 2.7 %collective-permute-start = (f32[4,2,32]{2,1,0:T(2,128)S(1)}, f32[4,2,32]{2,1,0:T(2,128)S(1)}, u32[]{:S(2)}, u32[]{:S(2)}) collective-permute-start(f32[4,2,32]{2,1,0:T(2,128)S(1)} %multiply_select_fusion.1), channel_id=1, source_target_pairs={{0,248},{8,0},{16,8},{24,16},{32,24},{40,32},{48,40},{56,48},{64,5... | collective-permute-start | bytes 3080 | tf_op jit(solution)/shard_map/ppermute | solution.py:15
  101.4 20.0 %collective-permute-start.2 = (f32[4,1,32,128]{2,1,0,3:T(1,128)S(1)}, f32[4,1,32,128]{2,1,0,3:T(1,128)S(1)}, u32[]{:S(2)}, u32[]{:S(2)}) collective-permute-start(f32[4,1,32,128]{2,1,0,3:T(1,128)S(1)} %get-tuple-element.86), channel_id=1, source_target_pairs={{0,1},{1,2},{2,3},{3,4},{4,5},{5,6},{6,7},{8,9},{9,10},{10,11},{11... | collective-permute-start | bytes 196616 | tf_op jit(solution)/shard_map/ppermute | solution.py:21
  121.4 1.2 copy-start.6
  122.7 4.1 %copy-start.9 = (f32[4,2,1,32,128]{4,3,2,1,0:T(8,128)S(1)}, f32[4,2,1,32,128]{4,3,2,1,0:T(8,128)}, u32[]{:S(2)}) copy-start(f32[4,2,1,32,128]{4,3,2,1,0:T(8,128)} %param.34) | copy-start | bytes 393220
  123.8 19.2 %collective-permute-start.4 = (f32[4,1,32,128]{2,1,0,3:T(1,128)S(1)}, f32[4,1,32,128]{2,1,0,3:T(1,128)S(1)}, u32[]{:S(2)}, u32[]{:S(2)}) collective-permute-start(f32[4,1,32,128]{2,1,0,3:T(1,128)S(1)} %get-tuple-element.82), channel_id=1, source_target_pairs={{1,0},{2,1},{3,2},{4,3},{5,4},{6,5},{7,6},{9,8},{10,9},{11,10},{12... | collective-permute-start | bytes 196616 | tf_op jit(solution)/shard_map/ppermute | solution.py:21
  127.2 16.6 %copy-start = (f32[4,1,32,128]{2,1,0,3:T(1,128)S(1)}, f32[4,1,32,128]{2,1,0,3:T(1,128)}, u32[]{:S(2)}) copy-start(f32[4,1,32,128]{2,1,0,3:T(1,128)} %get-tuple-element.81) | copy-start | bytes 196612
  127.2 16.6 %copy-start.2 = (f32[32,128]{0,1:T(8,128)S(1)}, f32[32,128]{0,1:T(8,128)}, u32[]{:S(2)}) copy-start(f32[32,128]{0,1:T(8,128)} %copy-done.1) | copy-start | bytes 49156
  143.1 0.7 copy-start.5
  147.5 0.8 copy-start.4
  147.5 3.5 %copy-start.3 = (f32[32,128]{0,1:T(8,128)S(1)}, f32[32,128]{0,1:T(8,128)}, u32[]{:S(2)}) copy-start(f32[32,128]{0,1:T(8,128)} %get-tuple-element.69) | copy-start | bytes 49156
  149.7 0.7 copy-start.21
  151.0 53.0 %collective-permute-start.3 = (f32[4,2,32]{2,1,0:T(2,128)}, f32[4,2,32]{2,1,0:T(2,128)S(1)}, u32[]{:S(2)}, u32[]{:S(2)}) collective-permute-start(f32[4,2,32]{2,1,0:T(2,128)} %multiply_select_fusion), channel_id=1, source_target_pairs={{0,248},{8,0},{16,8},{24,16},{32,24},{40,32},{48,40},{56,48},{64,5... | collective-permute-start | bytes 3080 | tf_op jit(solution)/shard_map/ppermute | solution.py:15
  152.1 0.7 copy-start.10
  152.1 0.7 copy-start.11
  200.1 14.7 %collective-permute-start.5 = (f32[4,1,32,128]{2,1,0,3:T(1,128)S(1)}, f32[4,1,32,128]{2,1,0,3:T(1,128)S(1)}, u32[]{:S(2)}, u32[]{:S(2)}) collective-permute-start(f32[4,1,32,128]{2,1,0,3:T(1,128)S(1)} %get-tuple-element.79), channel_id=1, source_target_pairs={{0,1},{1,2},{2,3},{3,4},{4,5},{5,6},{6,7},{8,9},{9,10},{10,11},{11... | collective-permute-start | bytes 196616 | tf_op jit(solution)/shard_map/ppermute | solution.py:21

commit v2 on v1

v2 whole, which is shorter than its diff:
```python
import jax
import jax.numpy as jnp
from jax import lax
from jax.experimental import pallas as pl
from jax.experimental.pallas import tpu as pltpu
from jax.sharding import PartitionSpec as P

FIELDS = 4
LEVELS_HERE = 2
PIECES = 3
ROWS_AT_ONCE = 8
MAP_HEIGHT, MAP_THERMAL, STEP_TWO, STEP_ONE, WEIGHTED, FLOW_TOP, STRETCH_TOP, STRETCH_NEXT, MIX_TOP = range(9)
SUMS = 9


def vmem(count):
    return [pl.BlockSpec(memory_space=pltpu.VMEM)] * count


def maps_kernel(records, thermal, elevation, out, total):
    sources, slots = records.shape[1:]
    rows, cols = thermal.shape
    half = jnp.bfloat16
    row_of = lax.broadcasted_iota(jnp.int32, (2 * rows, slots), 0).astype(jnp.float32).astype(half)
    col_of = lax.broadcasted_iota(jnp.int32, (cols, slots), 0).astype(jnp.float32).astype(half)
    nothing = jnp.zeros((2 * rows, slots), half)
    one, zero = jnp.ones((cols, slots), half), jnp.zeros((cols, slots), half)
    total[...] = jnp.zeros_like(total)

    def body(i, carry):
        left, right = [], []
        for j in range(ROWS_AT_ONCE):
            weight, scaled, kind, place = (records[n, pl.ds(i * ROWS_AT_ONCE + j, 1), :] for n in range(4))
            row = jnp.floor(place * (1.0 / cols))
            col = place - row * cols
            row = row + kind * rows
            here = jnp.broadcast_to(row.astype(half), nothing.shape) == row_of
            parts = []
            for rest in (weight, scaled):
                for _ in range(PIECES):
                    piece = rest.astype(half)
                    rest = rest - piece.astype(jnp.float32)
                    parts.append(jnp.where(here, jnp.broadcast_to(piece, nothing.shape), nothing))
            left.append(jnp.concatenate(parts, 0))
            right.append(jnp.where(jnp.broadcast_to(col.astype(half), one.shape) == col_of, one, zero))
        total[...] += lax.dot_general(
            jnp.concatenate(left, 1),
            jnp.concatenate(right, 1),
            (((1,), (1,)), ((), ())),
            preferred_element_type=jnp.float32,
        )
        return carry

    lax.fori_loop(0, sources // ROWS_AT_ONCE, body, 0)
    step = 2 * rows
    weights = sum(total[n * step : (n + 1) * step] for n in range(PIECES))
    values = sum(total[n * step : (n + 1) * step] for n in range(PIECES, 2 * PIECES))
    out[MAP_THERMAL] = thermal[...] * weights[:rows] - values[:rows]
    out[MAP_HEIGHT] = elevation[...] * weights[rows:] - values[rows:]


def local_maps(records, thermal, elevation):
    rows, cols = thermal.shape
    return pl.pallas_call(
        maps_kernel,
        out_shape=jax.ShapeDtypeStruct((2, rows, cols), jnp.float32),
        in_specs=vmem(3),
        out_specs=vmem(1)[0],
        scratch_shapes=[pltpu.VMEM((4 * PIECES * rows, cols), jnp.float32)],
        name="maps",
    )(records, thermal, elevation)


def along_columns(value, last):
    cols = value.shape[1]
    lane = lax.broadcasted_iota(jnp.int32, value.shape, 1)
    return jnp.where(lane == cols - 1, jnp.broadcast_to(last, value.shape), pltpu.roll(value, cols - 1, 1))


def across_rows(value, spread):
    rows = value.shape[0]
    face = spread * (pltpu.roll(value, rows - 1, 0) - value)
    return face - pltpu.roll(face, 1, 0)


def masked_spread(spread):
    row = lax.broadcasted_iota(jnp.int32, spread.shape, 0)
    return jnp.where(row < spread.shape[0] - 1, spread[...], 0.0)


def horizontal(value, flow, spread, last):
    scaled = flow * value
    return value + (along_columns(scaled, last) - scaled) + across_rows(value, spread)


def to_column(line, rows):
    wide = jnp.broadcast_to(line, (rows, line.shape[1]))
    same = lax.broadcasted_iota(jnp.int32, wide.shape, 0) == lax.broadcasted_iota(jnp.int32, wide.shape, 1)
    return jnp.sum(jnp.where(same, wide, 0.0), axis=1, keepdims=True)


def to_line(value, turned):
    rows = value.shape[0]
    row = lax.broadcasted_iota(jnp.int32, value.shape, 0)
    lane = lax.broadcasted_iota(jnp.int32, value.shape, 1)
    chosen = lane == jnp.where(turned, rows - 1 - row, row)
    return jnp.sum(jnp.where(chosen, jnp.broadcast_to(value[:, :1], value.shape), 0.0), axis=0, keepdims=True)


def edges(state, flow, turned, out):
    for k in range(LEVELS_HERE):
        lines = [to_line(flow[k] * state[f][k], turned) for f in range(FIELDS)]
        lines[2], lines[3] = jnp.where(turned, -lines[3], lines[2]), jnp.where(turned, lines[2], lines[3])
        for f in range(FIELDS):
            out[pl.ds(f * LEVELS_HERE + k, 1), :] = lines[f]


def start_kernel(flags, state, flow, mix, stretch, weight, halo, sums, edge):
    first = flags[0] == 0
    turned = flags[1] == 1
    maps = [[state[f, k] for k in range(LEVELS_HERE)] for f in range(FIELDS)]
    for f in range(FIELDS):
        for k in range(LEVELS_HERE):
            halo[k * FIELDS + f] = maps[f][k]
    halo[8] = weight[0]
    halo[9] = weight[1]
    halo[10] = mix[1]
    column = None
    for f in range(FIELDS):
        for k in range(LEVELS_HERE):
            term = stretch[f, k] * maps[f][k]
            column = term if column is None else column + term
    sums[0] = column
    sums[1] = stretch[2, 0] * weight[0] + stretch[2, 1] * weight[1]
    none = jnp.zeros_like(column)
    sums[2] = jnp.where(first, flow[0], none)
    sums[3] = jnp.where(first, stretch[0, 0], none)
    sums[4] = jnp.where(first, stretch[0, 1], none)
    sums[5] = jnp.where(first, mix[0], none)
    edges(maps, [flow[0], flow[1]], turned, edge)


def lower_mix(mix, flags):
    return jnp.where(flags[0] == flags[2], 0.0, mix[1])


def step_one_kernel(flags, state, flow, mix, stretch, spread, partner, relayed, edge, maps, sums, out):
    rows = spread.shape[0]
    low = flags[3] == 0
    spread_y = masked_spread(spread)
    mix_low = lower_mix(mix, flags)
    mix_high = jnp.where(low, relayed[5], partner[10])
    column = None
    for f in range(FIELDS):
        top, bottom = state[f, 0], state[f, 1]
        below = jnp.where(low, partner[f], relayed[f])
        above = jnp.where(low, relayed[f], partner[FIELDS + f])
        face = mix[0] * (bottom - top)
        new_top = horizontal(top, flow[0], spread_y, to_column(edge[2 * f : 2 * f + 1], rows))
        new_top = new_top + (face - mix_high * (top - above))
        new_bottom = horizontal(bottom, flow[1], spread_y, to_column(edge[2 * f + 1 : 2 * f + 2], rows))
        new_bottom = new_bottom + (mix_low * (below - bottom) - face)
        out[SUMS + f] = new_top
        out[SUMS + FIELDS + f] = new_bottom
        term = stretch[f, 0] * new_top + stretch[f, 1] * new_bottom
        column = term if column is None else column + term
    out[MAP_HEIGHT] = maps[MAP_HEIGHT]
    out[MAP_THERMAL] = maps[MAP_THERMAL]
    out[STEP_TWO] = column
    for n in range(SUMS - 3):
        out[STEP_ONE + n] = sums[n]


def middle_state(flags, own, sums, height, weight, mix, spread_y, last):
    first = flags[0] == 0
    thermal = sums[MAP_THERMAL]
    fields = [[own[k * FIELDS + f] for k in range(LEVELS_HERE)] for f in range(FIELDS)]
    moved = horizontal(thermal, sums[FLOW_TOP], spread_y, last) - sums[MIX_TOP] * thermal
    fields[0][0] = fields[0][0] + jnp.where(first, moved, 0.0)
    fields[0][1] = fields[0][1] + jnp.where(first, mix[0] * thermal, 0.0)
    for k in range(LEVELS_HERE):
        fields[2][k] = fields[2][k] + weight[k] * height
    return fields, moved


def edge_kernel(flags, own, sums, elevation, flow, mix, spread, weight, edge):
    turned = flags[1] == 1
    spread_y = masked_spread(spread)
    height = elevation[...] + sums[MAP_HEIGHT]
    fields, _ = middle_state(
        flags, own, sums, height, weight, mix, spread_y, jnp.zeros((spread.shape[0], 1), jnp.float32)
    )
    edges(fields, [flow[0], flow[1]], turned, edge)
    edge[8:16, :] = jnp.zeros((8, edge.shape[1]), jnp.float32)
    edge[8:9, :] = to_line(sums[FLOW_TOP] * sums[MAP_THERMAL], turned)


def step_two_kernel(
    flags, own, partner, relayed, sums, elevation, flow, mix, spread, weight,
    old_partner, old_relayed, edge, out_state, out_height,
):
    rows = spread.shape[0]
    low = flags[3] == 0
    spread_y = masked_spread(spread)
    mix_low = lower_mix(mix, flags)
    mix_high = jnp.where(low, old_relayed[5], old_partner[10])
    weight_above = jnp.where(low, old_relayed[4], old_partner[9])
    weight_below = jnp.where(low, old_partner[8], old_relayed[4])
    thermal = sums[MAP_THERMAL]
    height = elevation[...] + sums[MAP_HEIGHT]
    fields, moved = middle_state(
        flags, own, sums, height, weight, mix, spread_y, to_column(edge[8:9], rows)
    )
    height_one = height + sums[STEP_ONE] + sums[STRETCH_TOP] * thermal
    for f in range(FIELDS):
        top, bottom = fields[f]
        below = jnp.where(low, partner[f], relayed[f])
        above = jnp.where(low, relayed[f], partner[FIELDS + f])
        if f == 0:
            above = above + jnp.where(flags[0] == 1, sums[MIX_TOP] * thermal, 0.0)
        if f == 2:
            above = above + weight_above * height
            below = below + weight_below * height
        face = mix[0] * (bottom - top)
        new_top = horizontal(top, flow[0], spread_y, to_column(edge[2 * f : 2 * f + 1], rows))
        new_top = new_top + (face - mix_high * (top - above))
        new_bottom = horizontal(bottom, flow[1], spread_y, to_column(edge[2 * f + 1 : 2 * f + 2], rows))
        new_bottom = new_bottom + (mix_low * (below - bottom) - face)
        if f == 2:
            new_top = new_top + weight[0] * height_one
            new_bottom = new_bottom + weight[1] * height_one
        out_state[f, 0] = new_top
        out_state[f, 1] = new_bottom
    out_height[...] = (
        height_one
        + sums[STEP_TWO]
        + sums[WEIGHTED] * height
        + sums[STRETCH_TOP] * moved
        + sums[STRETCH_NEXT] * (sums[MIX_TOP] * thermal)
    )


def call(kernel, flags, operands, shapes, name):
    return pl.pallas_call(
        kernel,
        out_shape=[jax.ShapeDtypeStruct(shape, jnp.float32) for shape in shapes],
        in_specs=[pl.BlockSpec(memory_space=pltpu.SMEM)] + vmem(len(operands)),
        out_specs=vmem(len(shapes)),
        name=name,
    )(flags, *operands)


def per_device(
    costate_ending_fields,
    costate_ending_elevation,
    upstream_transport_coefficient,
    eastward_spread_coefficient,
    interface_blending_coefficient,
    thickness_sensitivity,
    layer_velocity_factor,
    western_join_turned,
    predicted_thermal_skin,
    predicted_elevation,
    measured_quantity,
    measurement_precision,
    measurement_sort,
    sampled_location,
    active_entry_numbers,
):
    rows = costate_ending_fields.shape[3]
    cols = costate_ending_fields.shape[4]
    slots = measured_quantity.shape[3]
    groups = lax.axis_size("lev")
    tiles = lax.axis_size("tile")
    lev_index = lax.axis_index("lev")
    tile_index = lax.axis_index("tile")
    low = lev_index % 2 == 0
    flip = [(l, l ^ 1) for l in range(groups)]
    pair = [(l, l ^ 2) for l in range(groups)]
    mirror = [(l, groups - 2 - (l & ~1) + (l & 1)) for l in range(groups)]
    relay = [(l, l + 2) for l in range(0, groups - 2, 2)] + [(l, l - 2) for l in range(3, groups, 2)]
    west = [(t, (t - 1) % tiles) for t in range(tiles)]
    flags = jnp.stack([lev_index, western_join_turned[tile_index], jnp.int32(groups - 1), lev_index % 2])

    state = costate_ending_fields[:, :, 0]
    elevation = costate_ending_elevation[0]
    flow = upstream_transport_coefficient[:, 0]
    spread = eastward_spread_coefficient[0]
    mix = interface_blending_coefficient[:, 0]
    stretch = thickness_sensitivity[:, :, 0]
    weight = layer_velocity_factor[:, 0]

    live = jnp.arange(slots, dtype=jnp.int32)[None, :] < active_entry_numbers[0, 0][:, None]
    precision = jnp.where(live, measurement_precision[0, 0], 0.0)
    packet = jnp.stack(
        [
            precision,
            precision * measured_quantity[0, 0],
            measurement_sort[0, 0].astype(jnp.float32),
            sampled_location[0, 0].astype(jnp.float32),
        ]
    )
    arrived = lax.all_to_all(packet, "tile", split_axis=1, concat_axis=1, tiled=True)

    halo, early, edge = call(
        start_kernel, flags, (state, flow, mix, stretch, weight),
        [(11, rows, cols), (SUMS - 3, rows, cols), (8, cols)], "start",
    )
    edge = lax.ppermute(edge, "tile", west)
    old_partner = lax.ppermute(halo, "lev", flip)
    passed = jnp.concatenate(
        [
            jnp.where(low, old_partner[FIELDS : 2 * FIELDS], old_partner[:FIELDS]),
            jnp.where(low, old_partner[9:10], old_partner[8:9]),
            old_partner[10:11],
        ]
    )
    old_relayed = lax.ppermute(passed, "lev", relay)

    maps = local_maps(arrived, predicted_thermal_skin[0], predicted_elevation[0])
    (mine,) = call(
        step_one_kernel, flags,
        (state, flow, mix, stretch, spread, old_partner, old_relayed, edge, maps, early),
        [(SUMS + 2 * FIELDS, rows, cols)], "step_one",
    )
    theirs = lax.ppermute(mine, "lev", flip)
    partner = theirs[SUMS:]
    relayed = lax.ppermute(jnp.where(low, partner[FIELDS:], partner[:FIELDS]), "lev", relay)
    sums = mine[:SUMS] + theirs[:SUMS]
    sums = sums + lax.ppermute(sums, "lev", pair)
    sums = sums + lax.ppermute(sums, "lev", mirror)
    own = mine[SUMS:]
    (edge,) = call(
        edge_kernel, flags, (own, sums, elevation, flow, mix, spread, weight), [(16, cols)], "edge"
    )
    edge = lax.ppermute(edge, "tile", west)
    out_state, out_height = call(
        step_two_kernel, flags,
        (own, partner, relayed, sums, elevation, flow, mix, spread, weight, old_partner, old_relayed, edge),
        [state.shape, (rows, cols)], "step_two",
    )
    return (out_state[:, :, None], out_height[None])


def solution(mesh):
    placed = (
        P(None, "lev", "tile", None, None),
        P("tile", None, None),
        P("lev", "tile", None, None),
        P("tile", None, None),
        P("lev", "tile", None, None),
        P(None, "lev", "tile", None, None),
        P("lev", "tile", None, None),
        P(),
        P("tile", None, None),
        P("tile", None, None),
        P("lev", "tile", None, None),
        P("lev", "tile", None, None),
        P("lev", "tile", None, None),
        P("lev", "tile", None, None),
        P("lev", "tile", None),
    )
    return jax.shard_map(
        per_device,
        mesh=mesh,
        in_specs=placed,
        out_specs=(P(None, "lev", "tile", None, None), P("tile", None, None)),
        check_vma=False,
    )
```

time: 220 us -> 82.1 us (0.37)
  the two profiles are of different devices: /device:TPU:38 before, /device:TPU:1 now
where the time goes in v2:
time: 82.1 us; the launch traced here: 81.6 us
  starting transfers between devices  30.6 us (37%)
  waiting for transfers between devices  25.5 us (31%)
  Pallas kernels  13.6 us (17%)
  local copies, waits for them, and re-layouts  6.93 us (8%)
  other arithmetic  4.05 us (5%)
  between operations  0.83 us (1%)
    ppermute x1, waiting for transfers between devices, per_device(): theirs = lax.ppermute(mine, 'lev', flip)  12.8 us
    pallas_call x4, Pallas kernels, call(): pl.pallas_call(kernel, out_shape=[jax.ShapeDtypeStruct(shape, jnp.float32...  8.02 us
    ppermute x1, starting transfers between devices, per_device(): old_partner = lax.ppermute(halo, 'lev', flip)  7.73 us
    all_to_all x1, starting transfers between devices, per_device(): lax.all_to_all(packet, 'tile', split_axis=1, concat_axis=1, tiled=True)  6.94 us
    all_to_all x1, waiting for transfers between devices, per_device(): lax.all_to_all(packet, 'tile', split_axis=1, concat_axis=1, tiled=True)  6.67 us
    pallas_call x1, Pallas kernels, local_maps(): pl.pallas_call(maps_kernel, out_shape=jax.ShapeDtypeStruct((2, rows, cols...  5.62 us
    ppermute x2, starting transfers between devices, per_device(): edge = lax.ppermute(edge, 'tile', west)  5.37 us
    ppermute x2, waiting for transfers between devices, per_device(): edge = lax.ppermute(edge, 'tile', west)  3.25 us
  transfers between devices with their start and end apart: 9, of which 4 were waited for; matrix products, arithmetic and copies ran while one was open for 6% of the time, Pallas kernels for 9%

profile of v2, /device:TPU:1, one launch (start us, length us, event | category | flops | bytes accessed | tf_op | source)
XLA Modules:
  0.0 81.6 jit_solution(12059871246364148722)
XLA Ops:
  0.7 0.6 copy-done.11
  1.3 0.6 dynamic_slice.3
  1.9 1.3 %pad_add_fusion.flags = s32[4]{0:T(128)} fusion(s32[1]{0:T(128)} %bitcast.1, s32[1]{0:T(128)} %constant.27.clone.1, s32[1]{0:T(128)} %dynamic_slice.3, s32[1]{0:T(128)} %bitcast), kind=kLoop, calls=%fused_computation.10 | loop fusion | flops 12 | bytes 32 | tf_op jit(solution)/shard_map/stack | solution.py:283
  3.1 1.7 %start.1 = (f32[11,32,128]{2,1,0:T(8,128)}, f32[6,32,128]{2,1,0:T(8,128)}, f32[8,128]{1,0:T(8,128)}) custom-call(s32[4]{0:T(128)} %pad_add_fusion.flags, f32[4,2,32,128]{3,2,1,0:T(8,128)} %bitcast.22, f32[2,32,128]{2,1,0:T(8,128)} %bitcast.26, f32[2,32,128]{2,1,0:T(8,128)} %bitcast.30, f32[4,2,32,128]{3,2,1,0:T(8,128)} %bitcast.24, f32[2,32,128]{2,1,0:T(8,128)} %bitcast.34), custom_call_target="tpu_custom_call" | custom-call | tf_op jit(solution)/shard_map/start/pallas_call | solution.py:244
  4.9 7.7 %collective-permute-start = (f32[11,32,128]{2,1,0:T(8,128)}, f32[11,32,128]{2,1,0:T(8,128)S(1)}, u32[]{:S(2)}, u32[]{:S(2)}) collective-permute-start(f32[11,32,128]{2,1,0:T(8,128)} %get-tuple-element.7), channel_id=1, source_target_pairs={{0,1},{1,0},{2,3},{3,2},{4,5},{5,4},{6,7},{7,6},{8,9},{9,8},{10,11... | collective-permute-start | bytes 540680 | tf_op jit(solution)/shard_map/ppermute | solution.py:310
  12.8 0.7 copy-done.5
  13.5 0.2 reshape_multiply_fusion
  13.7 1.0 %pad_maximum_fusion = f32[4,32,512]{2,0,1:T(4,128)} fusion(f32[1,32,512]{2,0,1:T(1,128)S(1)} %get-tuple-element.20, f32[1,32,512]{2,0,1:T(1,128)S(1)} %get-tuple-element.21, f32[1,32,512]{2,0,1:T(1,128)S(1)} %get-tuple-element.16, f32[1,32,512]{2,0,1:T(1,128)S(1)} %get-tuple-element.17), kind=kLoop, calls=%fused_computation | loop fusion | flops 196608 | bytes 524288 | tf_op jit(solution)/shard_map/stack | solution.py:295
  14.7 6.9 %all-to-all-start = ((f32[4,32,512]{2,0,1:T(4,128)}), f32[4,32,512]{2,0,1:T(4,128)S(1)}, u32[]{:S(2)}, u32[]{:S(2)}) async-start(f32[4,32,512]{2,0,1:T(4,128)} %pad_maximum_fusion), calls=%async_computation | async-start | bytes 524288 | tf_op jit(solution)/shard_map/all_to_all | solution.py:303
  21.7 0.6 copy-done
  22.3 3.1 %collective-permute-start.1 = (f32[6,32,128]{2,1,0:T(8,128)S(1)}, f32[6,32,128]{2,1,0:T(8,128)S(1)}, u32[]{:S(2)}, u32[]{:S(2)}) collective-permute-start(f32[6,32,128]{2,1,0:T(8,128)S(1)} %pad_maximum_fusion.1), channel_id=1, source_target_pairs={{0,2},{2,4},{4,6},{3,1},{5,3},{7,5},{8,10},{10,12},{12,14},{11,9},... | collective-permute-start | bytes 294920 | tf_op jit(solution)/shard_map/ppermute | solution.py:318
  25.4 0.6 collective-permute-start.2
  26.0 6.7 %all-to-all-done = f32[4,32,512]{2,0,1:T(4,128)S(1)} async-done(((f32[4,32,512]{2,0,1:T(4,128)}), f32[4,32,512]{2,0,1:T(4,128)S(1)}, u32[]{:S(2)}, u32[]{:S(2)}) %all-to-all-start) | async-done | bytes 262176 | tf_op jit(solution)/shard_map/all_to_all | solution.py:303
  32.7 0.8 copy.20.records
  33.5 5.6 %maps.1 = f32[2,32,128]{2,1,0:T(8,128)} custom-call(f32[4,32,512]{2,1,0:T(8,128)} %copy.20.records, f32[32,128]{1,0:T(8,128)} %bitcast.42, f32[32,128]{1,0:T(8,128)} %bitcast.43), custom_call_target="tpu_custom_call" | custom-call | tf_op jit(solution)/shard_map/maps/pallas_call | solution.py:64
  39.1 0.6 copy-done.8
  39.8 2.2 %step_one.1 = f32[17,32,128]{2,1,0:T(8,128)} custom-call(s32[4]{0:T(128)} %pad_add_fusion.flags, f32[4,2,32,128]{3,2,1,0:T(8,128)} %bitcast.23, f32[2,32,128]{2,1,0:T(8,128)} %bitcast.27, f32[2,32,128]{2,1,0:T(8,128)} %bitcast.31, f32[4,2,32,128]{3,2,1,0:T(8,128)} %bitcast.25, f32[32,128]{1,0:T(8,128)} %bitcast.37, f32[11,32,128]{2,1,0:T(8,128)} %copy-done, ...), custom_call_target="tpu_custom_call" | custom-call | tf_op jit(solution)/shard_map/step_one/pallas_call | solution.py:244
  42.0 1.8 %collective-permute-start.3 = (f32[17,32,128]{2,1,0:T(8,128)}, f32[17,32,128]{2,1,0:T(8,128)S(1)}, u32[]{:S(2)}, u32[]{:S(2)}) collective-permute-start(f32[17,32,128]{2,1,0:T(8,128)} %step_one.1), channel_id=1, source_target_pairs={{0,1},{1,0},{2,3},{3,2},{4,5},{5,4},{6,7},{7,6},{8,9},{9,8},{10,11... | collective-permute-start | bytes 835592 | tf_op jit(solution)/shard_map/ppermute | solution.py:326
  43.7 12.8 %collective-permute-done.3 = f32[17,32,128]{2,1,0:T(8,128)S(1)} collective-permute-done((f32[17,32,128]{2,1,0:T(8,128)}, f32[17,32,128]{2,1,0:T(8,128)S(1)}, u32[]{:S(2)}, u32[]{:S(2)}) %collective-permute-start.3) | collective-permute-done | bytes 278560 | tf_op jit(solution)/shard_map/ppermute | solution.py:326
  56.6 0.9 %slice_add_fusion = f32[9,32,128]{2,1,0:T(8,128)S(1)} fusion(f32[17,32,128]{2,1,0:T(8,128)S(1)} %collective-permute-done.3, f32[17,32,128]{2,1,0:T(8,128)} %step_one.1), kind=kLoop, calls=%fused_computation.2 | loop fusion | flops 36864 | bytes 442368 | tf_op jit(solution)/shard_map/add | solution.py:329
  57.5 1.3 %collective-permute-start.5 = (f32[9,32,128]{2,1,0:T(8,128)S(1)}, f32[9,32,128]{2,1,0:T(8,128)S(1)}, u32[]{:S(2)}, u32[]{:S(2)}) collective-permute-start(f32[9,32,128]{2,1,0:T(8,128)S(1)} %slice_add_fusion), channel_id=1, source_target_pairs={{0,2},{1,3},{2,0},{3,1},{4,6},{5,7},{6,4},{7,5},{8,10},{9,11},{10,... | collective-permute-start | bytes 442376 | tf_op jit(solution)/shard_map/ppermute | solution.py:330
  58.8 2.8 %collective-permute-done.5 = f32[9,32,128]{2,1,0:T(8,128)S(1)} collective-permute-done((f32[9,32,128]{2,1,0:T(8,128)S(1)}, f32[9,32,128]{2,1,0:T(8,128)S(1)}, u32[]{:S(2)}, u32[]{:S(2)}) %collective-permute-start.5) | collective-permute-done | bytes 147488 | tf_op jit(solution)/shard_map/ppermute | solution.py:330
  61.6 2.6 %collective-permute-start.6 = (f32[9,32,128]{2,1,0:T(8,128)S(1)}, f32[9,32,128]{2,1,0:T(8,128)S(1)}, u32[]{:S(2)}, u32[]{:S(2)}) collective-permute-start(f32[9,32,128]{2,1,0:T(8,128)S(1)} %add.20), channel_id=1, source_target_pairs={{0,6},{1,7},{2,4},{3,5},{4,2},{5,3},{6,0},{7,1},{8,14},{9,15},{10,... | collective-permute-start | bytes 442376 | tf_op jit(solution)/shard_map/ppermute | solution.py:331
  64.2 1.9 %collective-permute-start.4 = (f32[4,32,128]{2,1,0:T(8,128)S(1)}, f32[4,32,128]{2,1,0:T(8,128)S(1)}, u32[]{:S(2)}, u32[]{:S(2)}) collective-permute-start(f32[4,32,128]{2,1,0:T(8,128)S(1)} %slice_select_fusion), channel_id=1, source_target_pairs={{0,2},{2,4},{4,6},{3,1},{5,3},{7,5},{8,10},{10,12},{12,14},{11,9},... | collective-permute-start | bytes 196616 | tf_op jit(solution)/shard_map/ppermute | solution.py:328
  66.0 1.6 %slice.51.own = f32[8,32,128]{2,1,0:T(8,128)} slice(f32[17,32,128]{2,1,0:T(8,128)} %step_one.1), slice={[9:17], [0:32], [0:128]} | slice | bytes 262144 | tf_op jit(solution)/shard_map/slice | solution.py:332
  67.6 0.7 add.21.sums
  68.3 1.8 %edge.1 = f32[16,128]{1,0:T(8,128)} custom-call(s32[4]{0:T(128)} %pad_add_fusion.flags, f32[8,32,128]{2,1,0:T(8,128)} %slice.51.own, f32[9,32,128]{2,1,0:T(8,128)} %add.21.sums, f32[32,128]{1,0:T(8,128)} %bitcast.40, f32[2,32,128]{2,1,0:T(8,128)} %bitcast.28, f32[2,32,128]{2,1,0:T(8,128)} %bitcast.32, f32[32,128]{1,0:T(8,128)} %bitcast.38, ...), custom_call_target="tpu_custom_call" | custom-call | tf_op jit(solution)/shard_map/edge/pallas_call | solution.py:244
  70.1 4.8 %collective-permute-start.7 = (f32[16,128]{1,0:T(8,128)}, f32[16,128]{1,0:T(8,128)S(1)}, u32[]{:S(2)}, u32[]{:S(2)}) collective-permute-start(f32[16,128]{1,0:T(8,128)} %edge.1), channel_id=1, source_target_pairs={{0,248},{8,0},{16,8},{24,16},{32,24},{40,32},{48,40},{56,48},{64,5... | collective-permute-start | bytes 24584 | tf_op jit(solution)/shard_map/ppermute | solution.py:336
  74.9 0.6 slice.52.partner
  75.5 3.2 %collective-permute-done.7.edge = f32[16,128]{1,0:T(8,128)S(1)} collective-permute-done((f32[16,128]{1,0:T(8,128)}, f32[16,128]{1,0:T(8,128)S(1)}, u32[]{:S(2)}, u32[]{:S(2)}) %collective-permute-start.7) | collective-permute-done | bytes 8224 | tf_op jit(solution)/shard_map/ppermute | solution.py:336
  78.8 0.6 copy-done.7
  79.3 2.3 %step_two.1 = (f32[4,2,32,128]{3,2,1,0:T(8,128)}, f32[32,128]{1,0:T(8,128)}) custom-call(s32[4]{0:T(128)} %pad_add_fusion.flags, f32[8,32,128]{2,1,0:T(8,128)} %slice.51.own, f32[8,32,128]{2,1,0:T(8,128)} %slice.52.partner, f32[4,32,128]{2,1,0:T(8,128)} %copy-done.2, f32[9,32,128]{2,1,0:T(8,128)} %add.21.sums, f32[32,128]{1,0:T(8,128)} %bitcast.41, ...), custom_call_target="tpu_custom_call" | custom-call | tf_op jit(solution)/shard_map/step_two/pallas_call | solution.py:244
  (32 shorter events, 0.4 us)
Async XLA Ops:
  0.6 0.7 copy-start.11
  3.1 9.5 %copy-start.3 = (s32[1,1,32,512]{3,2,1,0:T(8,128)S(1)}, s32[1,1,32,512]{3,2,1,0:T(8,128)}, u32[]{:S(2)}) copy-start(s32[1,1,32,512]{3,2,1,0:T(8,128)} %param.27) | copy-start | bytes 196612
  4.9 7.7 %copy-start.4 = (s32[1,1,32,512]{3,2,1,0:T(8,128)S(1)}, s32[1,1,32,512]{3,2,1,0:T(8,128)}, u32[]{:S(2)}) copy-start(s32[1,1,32,512]{3,2,1,0:T(8,128)} %param.28) | copy-start | bytes 196612
  4.9 16.7 %collective-permute-start = (f32[11,32,128]{2,1,0:T(8,128)}, f32[11,32,128]{2,1,0:T(8,128)S(1)}, u32[]{:S(2)}, u32[]{:S(2)}) collective-permute-start(f32[11,32,128]{2,1,0:T(8,128)} %get-tuple-element.7), channel_id=1, source_target_pairs={{0,1},{1,0},{2,3},{3,2},{4,5},{5,4},{6,7},{7,6},{8,9},{9,8},{10,11... | collective-permute-start | bytes 540680 | tf_op jit(solution)/shard_map/ppermute | solution.py:310
  12.7 0.8 %copy-start.5 = (f32[1,1,32,512]{3,2,1,0:T(8,128)S(1)}, f32[1,1,32,512]{3,2,1,0:T(8,128)}, u32[]{:S(2)}) copy-start(f32[1,1,32,512]{3,2,1,0:T(8,128)} %param.25) | copy-start | bytes 196612
  12.7 0.9 %copy-start.6 = (f32[1,1,32,512]{3,2,1,0:T(8,128)S(1)}, f32[1,1,32,512]{3,2,1,0:T(8,128)}, u32[]{:S(2)}) copy-start(f32[1,1,32,512]{3,2,1,0:T(8,128)} %param.26) | copy-start | bytes 196612
  12.8 0.7 copy-start.9
  14.7 18.0 %all-to-all-start = ((f32[4,32,512]{2,0,1:T(4,128)}), f32[4,32,512]{2,0,1:T(4,128)S(1)}, u32[]{:S(2)}, u32[]{:S(2)}) async-start(f32[4,32,512]{2,0,1:T(4,128)} %pad_maximum_fusion), calls=%async_computation | async-start | bytes 524288 | tf_op jit(solution)/shard_map/all_to_all | solution.py:303
  21.6 0.7 copy-start
  21.7 3.7 %copy-start.10 = (f32[8,128]{1,0:T(8,128)S(1)}, f32[8,128]{1,0:T(8,128)}, u32[]{:S(2)}) copy-start(f32[8,128]{1,0:T(8,128)} %get-tuple-element.8) | copy-start | bytes 12292
  22.3 16.8 %collective-permute-start.1 = (f32[6,32,128]{2,1,0:T(8,128)S(1)}, f32[6,32,128]{2,1,0:T(8,128)S(1)}, u32[]{:S(2)}, u32[]{:S(2)}) collective-permute-start(f32[6,32,128]{2,1,0:T(8,128)S(1)} %pad_maximum_fusion.1), channel_id=1, source_target_pairs={{0,2},{2,4},{4,6},{3,1},{5,3},{7,5},{8,10},{10,12},{12,14},{11,9},... | collective-permute-start | bytes 294920 | tf_op jit(solution)/shard_map/ppermute | solution.py:318
  25.4 13.7 %collective-permute-start.2 = (f32[8,128]{1,0:T(8,128)S(1)}, f32[8,128]{1,0:T(8,128)S(1)}, u32[]{:S(2)}, u32[]{:S(2)}) collective-permute-start(f32[8,128]{1,0:T(8,128)S(1)} %copy-done.10), channel_id=1, source_target_pairs={{0,248},{8,0},{16,8},{24,16},{32,24},{40,32},{48,40},{56,48},{64,5... | collective-permute-start | bytes 12296 | tf_op jit(solution)/shard_map/ppermute | solution.py:309
  39.1 0.6 copy-start.8
  39.1 0.6 copy-start.1
  42.0 14.6 %collective-permute-start.3 = (f32[17,32,128]{2,1,0:T(8,128)}, f32[17,32,128]{2,1,0:T(8,128)S(1)}, u32[]{:S(2)}, u32[]{:S(2)}) collective-permute-start(f32[17,32,128]{2,1,0:T(8,128)} %step_one.1), channel_id=1, source_target_pairs={{0,1},{1,0},{2,3},{3,2},{4,5},{5,4},{6,7},{7,6},{8,9},{9,8},{10,11... | collective-permute-start | bytes 835592 | tf_op jit(solution)/shard_map/ppermute | solution.py:326
  57.5 4.1 %collective-permute-start.5 = (f32[9,32,128]{2,1,0:T(8,128)S(1)}, f32[9,32,128]{2,1,0:T(8,128)S(1)}, u32[]{:S(2)}, u32[]{:S(2)}) collective-permute-start(f32[9,32,128]{2,1,0:T(8,128)S(1)} %slice_add_fusion), channel_id=1, source_target_pairs={{0,2},{1,3},{2,0},{3,1},{4,6},{5,7},{6,4},{7,5},{8,10},{9,11},{10,... | collective-permute-start | bytes 442376 | tf_op jit(solution)/shard_map/ppermute | solution.py:330
  61.6 6.0 %collective-permute-start.6 = (f32[9,32,128]{2,1,0:T(8,128)S(1)}, f32[9,32,128]{2,1,0:T(8,128)S(1)}, u32[]{:S(2)}, u32[]{:S(2)}) collective-permute-start(f32[9,32,128]{2,1,0:T(8,128)S(1)} %add.20), channel_id=1, source_target_pairs={{0,6},{1,7},{2,4},{3,5},{4,2},{5,3},{6,0},{7,1},{8,14},{9,15},{10,... | collective-permute-start | bytes 442376 | tf_op jit(solution)/shard_map/ppermute | solution.py:331
  64.2 11.3 %collective-permute-start.4 = (f32[4,32,128]{2,1,0:T(8,128)S(1)}, f32[4,32,128]{2,1,0:T(8,128)S(1)}, u32[]{:S(2)}, u32[]{:S(2)}) collective-permute-start(f32[4,32,128]{2,1,0:T(8,128)S(1)} %slice_select_fusion), channel_id=1, source_target_pairs={{0,2},{2,4},{4,6},{3,1},{5,3},{7,5},{8,10},{10,12},{12,14},{11,9},... | collective-permute-start | bytes 196616 | tf_op jit(solution)/shard_map/ppermute | solution.py:328
  70.1 8.7 %collective-permute-start.7 = (f32[16,128]{1,0:T(8,128)}, f32[16,128]{1,0:T(8,128)S(1)}, u32[]{:S(2)}, u32[]{:S(2)}) collective-permute-start(f32[16,128]{1,0:T(8,128)} %edge.1), channel_id=1, source_target_pairs={{0,248},{8,0},{16,8},{24,16},{32,24},{40,32},{48,40},{56,48},{64,5... | collective-permute-start | bytes 24584 | tf_op jit(solution)/shard_map/ppermute | solution.py:336
  75.5 3.2 %copy-start.2 = (f32[4,32,128]{2,1,0:T(8,128)}, f32[4,32,128]{2,1,0:T(8,128)S(1)}, u32[]{:S(2)}) copy-start(f32[4,32,128]{2,1,0:T(8,128)S(1)} %collective-permute-done.4.relayed) | copy-start | bytes 196612
  78.8 0.6 copy-start.7

commit v3 on v1

v3 whole, which is shorter than its diff:
```python
import jax
import jax.numpy as jnp
from jax import lax
from jax.experimental import pallas as pl
from jax.experimental.pallas import tpu as pltpu
from jax.sharding import PartitionSpec as P

FIELDS = 4
LEVELS_HERE = 2
PIECES = 3
ROWS_AT_ONCE = 8
MAP_HEIGHT, MAP_THERMAL, STEP_TWO = range(3)
STEP_ONE, WEIGHTED, FLOW_TOP, STRETCH_TOP, THERMAL_GAIN = range(5)
EARLY = 5
HALO, MIDDLE = FIELDS + 1, FIELDS + 2


def maps_kernel(records, thermal, elevation, out, total):
    rows, cols = thermal.shape
    sources, _, slots = records.shape
    half = jnp.bfloat16
    row_of = lax.broadcasted_iota(jnp.int32, (2 * rows, slots), 0).astype(jnp.float32).astype(half)
    col_of = lax.broadcasted_iota(jnp.int32, (cols, slots), 0).astype(jnp.float32).astype(half)
    nothing = jnp.zeros((2 * rows, slots), half)
    one, zero = jnp.ones((cols, slots), half), jnp.zeros((cols, slots), half)
    total[...] = jnp.zeros_like(total)

    def body(i, carry):
        left, right = [], []
        for j in range(ROWS_AT_ONCE):
            weight, scaled, kind, place = (
                records[i * ROWS_AT_ONCE + j, n : n + 1, :] for n in range(4)
            )
            row = jnp.floor(place * (1.0 / cols))
            col = place - row * cols
            row = row + kind * rows
            here = jnp.broadcast_to(row.astype(half), nothing.shape) == row_of
            parts = []
            for rest in (weight, scaled):
                for _ in range(PIECES):
                    piece = rest.astype(half)
                    rest = rest - piece.astype(jnp.float32)
                    parts.append(jnp.where(here, jnp.broadcast_to(piece, nothing.shape), nothing))
            left.append(jnp.concatenate(parts, 0))
            right.append(jnp.where(jnp.broadcast_to(col.astype(half), one.shape) == col_of, one, zero))
        total[...] += lax.dot_general(
            jnp.concatenate(left, 1),
            jnp.concatenate(right, 1),
            (((1,), (1,)), ((), ())),
            preferred_element_type=jnp.float32,
        )
        return carry

    lax.fori_loop(0, sources // ROWS_AT_ONCE, body, 0)
    step = 2 * rows
    weights = sum(total[n * step : (n + 1) * step] for n in range(PIECES))
    values = sum(total[n * step : (n + 1) * step] for n in range(PIECES, 2 * PIECES))
    out[MAP_THERMAL] = thermal[...] * weights[:rows] - values[:rows]
    out[MAP_HEIGHT] = elevation[...] * weights[rows:] - values[rows:]


def place(turned_ref):
    lev = lax.axis_index("lev")
    turned = turned_ref[lax.axis_index("tile")] == 1
    return lev, lev == lax.axis_size("lev") - 1, lev % 2 == 0, turned


def along_columns(value, last):
    cols = value.shape[1]
    lane = lax.broadcasted_iota(jnp.int32, value.shape, 1)
    return jnp.where(lane == cols - 1, jnp.broadcast_to(last, value.shape), pltpu.roll(value, cols - 1, 1))


def across_rows(value, spread):
    rows = value.shape[0]
    face = spread * (pltpu.roll(value, rows - 1, 0) - value)
    return face - pltpu.roll(face, 1, 0)


def masked_spread(spread):
    row = lax.broadcasted_iota(jnp.int32, spread.shape, 0)
    return jnp.where(row < spread.shape[0] - 1, spread[...], 0.0)


def horizontal(value, flow, spread, last):
    scaled = flow * value
    return value + (along_columns(scaled, last) - scaled) + across_rows(value, spread)


def to_column(line, rows, shift):
    wide = jnp.broadcast_to(line, (rows, line.shape[1]))
    row = lax.broadcasted_iota(jnp.int32, wide.shape, 0)
    lane = lax.broadcasted_iota(jnp.int32, wide.shape, 1)
    return jnp.sum(jnp.where(lane == row + shift, wide, 0.0), axis=1, keepdims=True)


def to_line(value, turned, shift):
    rows = value.shape[0]
    row = lax.broadcasted_iota(jnp.int32, value.shape, 0)
    lane = lax.broadcasted_iota(jnp.int32, value.shape, 1)
    chosen = lane == shift + jnp.where(turned, rows - 1 - row, row)
    return jnp.sum(jnp.where(chosen, jnp.broadcast_to(value[:, :1], value.shape), 0.0), axis=0, keepdims=True)


def edges(state, flow, turned):
    rows = state[0][0].shape[0]
    lines = [
        sum(to_line(flow[k] * state[f][k], turned, k * rows) for k in range(LEVELS_HERE)) for f in range(FIELDS)
    ]
    lines[2], lines[3] = jnp.where(turned, -lines[3], lines[2]), jnp.where(turned, lines[2], lines[3])
    return lines


def store_lines(lines, out):
    rest = jnp.zeros((out.shape[0] - len(lines), out.shape[1]), jnp.float32)
    out[...] = jnp.concatenate([*lines, rest], 0)


def packet_kernel(counts, measured, precision, kind, location, packet):
    sources, slots = measured.shape
    lane = lax.broadcasted_iota(jnp.int32, (1, slots), 1)
    for s in range(sources):
        weight = jnp.where(lane < counts[s], precision[s : s + 1, :], 0.0)
        packet[s, 0:1, :] = weight
        packet[s, 1:2, :] = weight * measured[s : s + 1, :]
        packet[s, 2:3, :] = kind[s : s + 1, :].astype(jnp.float32)
        packet[s, 3:4, :] = location[s : s + 1, :].astype(jnp.float32)


def start_kernel(turned_ref, state, flow, mix, stretch, weight, to_flip, to_other, early, edge):
    lev, _, low, turned = place(turned_ref)
    first = lev == 0
    column = None
    for f in range(FIELDS):
        top, bottom = state[f, 0], state[f, 1]
        to_flip[f] = jnp.where(low, bottom, top)
        to_other[f] = jnp.where(low, top, bottom)
        term = stretch[f, 0] * top + stretch[f, 1] * bottom
        column = term if column is None else column + term
    to_flip[FIELDS] = mix[1]
    to_other[FIELDS] = mix[1]
    none = jnp.zeros_like(column)
    gain = stretch[0, 0] * (1.0 - flow[0] - mix[0]) + stretch[0, 1] * mix[0]
    early[STEP_ONE] = column
    early[WEIGHTED] = stretch[2, 0] * weight[0] + stretch[2, 1] * weight[1]
    early[FLOW_TOP] = jnp.where(first, flow[0], none)
    early[STRETCH_TOP] = jnp.where(first, stretch[0, 0], none)
    early[THERMAL_GAIN] = jnp.where(first, gain, none)
    store_lines(
        edges([[state[f, k] for k in range(LEVELS_HERE)] for f in range(FIELDS)], [flow[0], flow[1]], turned), edge
    )


def step(fields, flow, mix, mix_low, mix_high, spread_y, lines, above, below):
    rows = spread_y.shape[0]
    for f in range(FIELDS):
        top, bottom = fields(f)
        face = mix[0] * (bottom - top)
        new_top = horizontal(top, flow[0], spread_y, to_column(lines[f : f + 1, :], rows, 0))
        new_top = new_top + (face - mix_high * (top - above(f)))
        new_bottom = horizontal(bottom, flow[1], spread_y, to_column(lines[f : f + 1, :], rows, rows))
        new_bottom = new_bottom + (mix_low * (below(f) - bottom) - face)
        yield f, new_top, new_bottom


def step_one_kernel(
    turned_ref, state, flow, mix, stretch, spread, weight, flipped, crossed, edge, early,
    own, to_flip, to_other, column_out,
):
    _, last, low, _ = place(turned_ref)
    mix_low = jnp.where(last, 0.0, mix[1])
    mix_high = jnp.where(low, crossed[FIELDS], flipped[FIELDS])
    column = None
    for f, top, bottom in step(
        lambda f: (state[f, 0], state[f, 1]), flow, mix, mix_low, mix_high, masked_spread(spread), edge,
        lambda f: jnp.where(low, crossed[f], flipped[f]),
        lambda f: jnp.where(low, flipped[f], crossed[f]),
    ):
        own[f, 0] = top
        own[f, 1] = bottom
        to_flip[f] = jnp.where(low, bottom, top)
        to_other[f] = jnp.where(low, top, bottom)
        term = stretch[f, 0] * top + stretch[f, 1] * bottom
        column = term if column is None else column + term
    to_flip[FIELDS] = jnp.where(low, weight[1], weight[0])
    to_other[FIELDS] = jnp.where(low, weight[0], weight[1])
    to_flip[FIELDS + 1] = mix[0]
    to_other[FIELDS + 1] = mix[0]
    for n in range(EARLY):
        to_flip[MIDDLE + n] = early[n]
    column_out[0] = column


def middle_state(first, own, thermal, height, flow, weight, mix, spread_y, last):
    fields = [[own[f, k] for k in range(LEVELS_HERE)] for f in range(FIELDS)]
    moved = horizontal(thermal, flow[0], spread_y, last) - mix[0] * thermal
    fields[0][0] = fields[0][0] + jnp.where(first, moved, 0.0)
    fields[0][1] = fields[0][1] + jnp.where(first, mix[0] * thermal, 0.0)
    for k in range(LEVELS_HERE):
        fields[2][k] = fields[2][k] + weight[k] * height
    return fields


def edge_kernel(turned_ref, own, half, other, early, flipped, elevation, flow, mix, spread, weight, edge):
    lev, _, _, turned = place(turned_ref)
    rows = spread.shape[0]
    height = elevation[...] + (half[MAP_HEIGHT] + other[MAP_HEIGHT])
    thermal = half[MAP_THERMAL] + other[MAP_THERMAL]
    flow_top = early[FLOW_TOP] + flipped[MIDDLE + FLOW_TOP]
    fields = middle_state(
        lev == 0, own, thermal, height, flow, weight, mix, masked_spread(spread), jnp.zeros((rows, 1), jnp.float32)
    )
    lines = edges(fields, [flow[0], flow[1]], turned)
    lines.append(to_line(flow_top * thermal, turned, 0))
    store_lines(lines, edge)


def step_two_kernel(
    turned_ref, own, half, other, early, column, column_other, elevation, flow, mix, spread, weight,
    flipped, crossed, old_flipped, old_crossed, edge, out_state, out_height,
):
    lev, last, low, _ = place(turned_ref)
    rows = spread.shape[0]
    spread_y = masked_spread(spread)
    mix_low = jnp.where(last, 0.0, mix[1])
    mix_high = jnp.where(low, old_crossed[FIELDS], old_flipped[FIELDS])
    weight_above = jnp.where(low, crossed[FIELDS], flipped[FIELDS])
    weight_below = jnp.where(low, flipped[FIELDS], crossed[FIELDS])

    def total(n):
        return early[n] + flipped[MIDDLE + n]

    thermal = half[MAP_THERMAL] + other[MAP_THERMAL]
    height = elevation[...] + (half[MAP_HEIGHT] + other[MAP_HEIGHT])
    stretch_top = total(STRETCH_TOP)
    seam = to_column(edge[FIELDS : FIELDS + 1, :], rows, 0)
    fields = middle_state(lev == 0, own, thermal, height, flow, weight, mix, spread_y, seam)
    height_one = height + total(STEP_ONE) + stretch_top * thermal

    def above(f):
        value = jnp.where(low, crossed[f], flipped[f])
        if f == 0:
            value = value + jnp.where(lev == 1, flipped[FIELDS + 1] * thermal, 0.0)
        return value + weight_above * height if f == 2 else value

    def below(f):
        value = jnp.where(low, flipped[f], crossed[f])
        return value + weight_below * height if f == 2 else value

    for f, top, bottom in step(
        lambda f: fields[f], flow, mix, mix_low, mix_high, spread_y, edge, above, below
    ):
        out_state[f, 0] = top + weight[0] * height_one if f == 2 else top
        out_state[f, 1] = bottom + weight[1] * height_one if f == 2 else bottom
    out_height[...] = (
        height_one
        + (column[0] + column_other[0])
        + total(WEIGHTED) * height
        + total(THERMAL_GAIN) * thermal
        + stretch_top * (along_columns(total(FLOW_TOP) * thermal, seam) + across_rows(thermal, spread_y))
    )


def call(kernel, operands, shapes, smem=(), scratch=(), grant=16 << 20):
    count, outs = len(operands), len(shapes)

    def body(*refs):
        scalars, refs = refs[: len(smem)], refs[len(smem) :]
        sources, refs = refs[:count], refs[count:]
        results, refs = refs[:outs], refs[outs:]
        held, semaphores, rest = refs[:count], refs[count], refs[count + 1 :]
        copies = [pltpu.make_async_copy(s, h, semaphores.at[n]) for n, (s, h) in enumerate(zip(sources, held))]
        for copy in copies:
            copy.start()
        for copy in copies:
            copy.wait()
        kernel(*scalars, *held, *results, *rest)

    return pl.pallas_call(
        body,
        out_shape=[jax.ShapeDtypeStruct(shape, jnp.float32) for shape in shapes],
        in_specs=[pl.BlockSpec(memory_space=pltpu.SMEM)] * len(smem) + [pl.BlockSpec(memory_space=pl.ANY)] * count,
        out_specs=[pl.BlockSpec(memory_space=pltpu.VMEM)] * outs,
        scratch_shapes=[
            *(pltpu.VMEM(o.shape, o.dtype) for o in operands),
            pltpu.SemaphoreType.DMA((count,)),
            *scratch,
        ],
        compiler_params=pltpu.CompilerParams(vmem_limit_bytes=grant),
    )(*smem, *operands)


def per_device(
    costate_ending_fields,
    costate_ending_elevation,
    upstream_transport_coefficient,
    eastward_spread_coefficient,
    interface_blending_coefficient,
    thickness_sensitivity,
    layer_velocity_factor,
    western_join_turned,
    predicted_thermal_skin,
    predicted_elevation,
    measured_quantity,
    measurement_precision,
    measurement_sort,
    sampled_location,
    active_entry_numbers,
):
    rows = costate_ending_fields.shape[3]
    cols = costate_ending_fields.shape[4]
    slots = measured_quantity.shape[3]
    groups = lax.axis_size("lev")
    tiles = lax.axis_size("tile")
    flip = [(l, l ^ 1) for l in range(groups)]
    cross = [(l, l + 1) for l in range(1, groups - 1, 2)] + [(l + 1, l) for l in range(1, groups - 1, 2)]
    pair = [(l, l ^ 2) for l in range(groups)]
    mirror = [(l, groups - 2 - (l & ~1) + (l & 1)) for l in range(groups)]
    west = [(t, (t - 1) % tiles) for t in range(tiles)]
    turned = western_join_turned

    state = costate_ending_fields[:, :, 0]
    elevation = costate_ending_elevation[0]
    flow = upstream_transport_coefficient[:, 0]
    spread = eastward_spread_coefficient[0]
    mix = interface_blending_coefficient[:, 0]
    stretch = thickness_sensitivity[:, :, 0]
    weight = layer_velocity_factor[:, 0]

    field = (rows, cols)
    (packet,) = call(
        packet_kernel,
        (measured_quantity[0, 0], measurement_precision[0, 0], measurement_sort[0, 0], sampled_location[0, 0]),
        [(tiles, 4, slots)], smem=(active_entry_numbers[0, 0],), grant=60 * 1024 * 1024,
    )
    arrived = lax.all_to_all(packet, "tile", split_axis=0, concat_axis=0, tiled=True)

    to_flip, to_other, early, edge = call(
        start_kernel, (state, flow, mix, stretch, weight),
        [(HALO, *field), (HALO, *field), (EARLY, *field), (8, cols)], smem=(turned,),
    )
    early = early + lax.ppermute(early, "lev", pair)
    old_flipped = lax.ppermute(to_flip, "lev", flip)
    old_crossed = lax.ppermute(to_other, "lev", cross)
    edge = lax.ppermute(edge, "tile", west)
    early = early + lax.ppermute(early, "lev", mirror)
    (sums,) = call(
        maps_kernel, (arrived, predicted_thermal_skin[0], predicted_elevation[0]),
        [(2, *field)], scratch=[pltpu.VMEM((4 * PIECES * rows, cols), jnp.float32)],
    )
    sums = sums + lax.ppermute(sums, "lev", pair)
    own, to_flip, to_other, column = call(
        step_one_kernel,
        (state, flow, mix, stretch, spread, weight, old_flipped, old_crossed, edge, early),
        [state.shape, (MIDDLE + EARLY, *field), (MIDDLE, *field), (1, *field)], smem=(turned,),
    )
    both = jnp.concatenate([sums, column])
    both = both + lax.ppermute(both, "lev", mirror)
    flipped = lax.ppermute(to_flip, "lev", flip)
    other = lax.ppermute(both, "lev", flip)
    crossed = lax.ppermute(to_other, "lev", cross)
    column = both[STEP_TWO:] + other[STEP_TWO:]
    column_other = lax.ppermute(column, "lev", pair)
    (edge,) = call(
        edge_kernel, (own, both, other, early, flipped, elevation, flow, mix, spread, weight),
        [(8, cols)], smem=(turned,),
    )
    edge = lax.ppermute(edge, "tile", west)
    out_state, out_height = call(
        step_two_kernel,
        (own, both, other, early, column, column_other, elevation, flow, mix, spread, weight,
         flipped, crossed, old_flipped, old_crossed, edge),
        [state.shape, field], smem=(turned,),
    )
    return (out_state[:, :, None], out_height[None])


def solution(mesh):
    placed = (
        P(None, "lev", "tile", None, None),
        P("tile", None, None),
        P("lev", "tile", None, None),
        P("tile", None, None),
        P("lev", "tile", None, None),
        P(None, "lev", "tile", None, None),
        P("lev", "tile", None, None),
        P(),
        P("tile", None, None),
        P("tile", None, None),
        P("lev", "tile", None, None),
        P("lev", "tile", None, None),
        P("lev", "tile", None, None),
        P("lev", "tile", None, None),
        P("lev", "tile", None),
    )
    return jax.shard_map(
        per_device,
        mesh=mesh,
        in_specs=placed,
        out_specs=(P(None, "lev", "tile", None, None), P("tile", None, None)),
        check_vma=False,
    )
```

time: 220 us -> 78.4 us (0.36)
  the two profiles are of different devices: /device:TPU:38 before, /device:TPU:2 now
where the time goes in v3:
time: 78.4 us; the launch traced here: 78.1 us
  starting transfers between devices  42.1 us (54%)
  waiting for transfers between devices  20.3 us (26%)
  Pallas kernels  14 us (18%)
  between operations  0.88 us (1%)
    pallas_call x6, Pallas kernels, call(): pl.pallas_call(body, out_shape=[jax.ShapeDtypeStruct(shape, jnp.float32)...  14 us
    ppermute x1, waiting for transfers between devices, per_device(): flipped = lax.ppermute(to_flip, 'lev', flip)  9.86 us
    all_to_all x1, starting transfers between devices, per_device(): lax.all_to_all(packet, 'tile', split_axis=0, concat_axis=0, tiled=True)  9.06 us
    ppermute x2, starting transfers between devices, per_device(): edge = lax.ppermute(edge, 'tile', west)  7.38 us
    ppermute x1, starting transfers between devices, per_device(): crossed = lax.ppermute(to_other, 'lev', cross)  5.79 us
    ppermute x1, starting transfers between devices, per_device(): old_crossed = lax.ppermute(to_other, 'lev', cross)  4.58 us
    ppermute x1, starting transfers between devices, per_device(): old_flipped = lax.ppermute(to_flip, 'lev', flip)  4.49 us
    ppermute x1, starting transfers between devices, per_device(): other = lax.ppermute(both, 'lev', flip)  4.42 us
  transfers between devices with their start and end apart: 13, of which 5 were waited for; matrix products, arithmetic and copies ran while one was open for 0% of the time, Pallas kernels for 11%

profile of v3, /device:TPU:2, one launch (start us, length us, event | category | flops | bytes accessed | tf_op | source)
XLA Modules:
  0.0 78.1 jit_solution(7213932225483867579)
XLA Ops:
  0.6 2.5 %shard_map.160 = f32[32,4,512]{2,1,0:T(4,128)} custom-call(s32[32]{0:T(128)} %bitcast.45, f32[32,512]{1,0:T(8,128)} %bitcast.41, f32[32,512]{1,0:T(8,128)} %bitcast.42, s32[32,512]{1,0:T(8,128)} %bitcast.43, s32[32,512]{1,0:T(8,128)} %bitcast.44), custom_call_target="tpu_custom_call" | custom-call | tf_op jit(solution)/shard_map/pallas_call | solution.py:279
  3.1 0.0 copy-start
  3.1 0.0 copy-start.1
  3.1 0.0 copy-start.2
  3.1 0.0 copy-start.3
  3.1 0.0 copy-start.4
  3.2 9.1 %all-to-all-start = ((f32[32,4,512]{2,1,0:T(4,128)}), f32[32,4,512]{2,1,0:T(4,128)S(1)}, u32[]{:S(2)}, u32[]{:S(2)}) async-start(f32[32,4,512]{2,1,0:T(4,128)} %shard_map.160), calls=%async_computation | async-start | bytes 524288 | tf_op jit(solution)/shard_map/all_to_all | solution.py:336
  12.3 0.6 copy-done.9
  12.9 1.2 %shard_map.158 = (f32[5,32,128]{2,1,0:T(8,128)S(1)}, f32[5,32,128]{2,1,0:T(8,128)S(1)}, f32[5,32,128]{2,1,0:T(8,128)S(1)}, f32[8,128]{1,0:T(8,128)S(1)}) custom-call(s32[32]{0:T(128)S(1)} %copy-done.9, f32[4,2,32,128]{3,2,1,0:T(8,128)S(1)} %bitcast.30, f32[2,32,128]{2,1,0:T(8,128)S(1)} %bitcast.18, f32[2,32,128]{2,1,0:T(8,128)S(1)} %bitcast.22, ...), custom_call_target="tpu_custom_call" | custom-call | tf_op jit(solution)/shard_map/pallas_call | solution.py:279
  14.1 0.6 collective-permute-start.3
  14.7 4.1 %collective-permute-done.3 = f32[5,32,128]{2,1,0:T(8,128)S(1)} collective-permute-done((f32[5,32,128]{2,1,0:T(8,128)S(1)}, f32[5,32,128]{2,1,0:T(8,128)S(1)}, u32[]{:S(2)}, u32[]{:S(2)}) %collective-permute-start.3) | collective-permute-done | bytes 81952 | tf_op jit(solution)/shard_map/ppermute | solution.py:342
  18.8 1.6 %collective-permute-start.4 = (f32[5,32,128]{2,1,0:T(8,128)S(1)}, f32[5,32,128]{2,1,0:T(8,128)S(1)}, u32[]{:S(2)}, u32[]{:S(2)}) collective-permute-start(f32[5,32,128]{2,1,0:T(8,128)S(1)} %add.15), channel_id=1, source_target_pairs={{0,6},{1,7},{2,4},{3,5},{4,2},{5,3},{6,0},{7,1},{8,14},{9,15},{10,... | collective-permute-start | bytes 245768 | tf_op jit(solution)/shard_map/ppermute | solution.py:346
  20.4 4.5 %collective-permute-start = (f32[5,32,128]{2,1,0:T(8,128)S(1)}, f32[5,32,128]{2,1,0:T(8,128)S(1)}, u32[]{:S(2)}, u32[]{:S(2)}) collective-permute-start(f32[5,32,128]{2,1,0:T(8,128)S(1)} %get-tuple-element.12), channel_id=1, source_target_pairs={{0,1},{1,0},{2,3},{3,2},{4,5},{5,4},{6,7},{7,6},{8,9},{9,8},{10,11... | collective-permute-start | bytes 245768 | tf_op jit(solution)/shard_map/ppermute | solution.py:343
  24.9 4.6 %collective-permute-start.1 = (f32[5,32,128]{2,1,0:T(8,128)S(1)}, f32[5,32,128]{2,1,0:T(8,128)S(1)}, u32[]{:S(2)}, u32[]{:S(2)}) collective-permute-start(f32[5,32,128]{2,1,0:T(8,128)S(1)} %get-tuple-element.13), channel_id=1, source_target_pairs={{1,2},{3,4},{5,6},{2,1},{4,3},{6,5},{9,10},{11,12},{13,14},{10,9},... | collective-permute-start | bytes 245768 | tf_op jit(solution)/shard_map/ppermute | solution.py:344
  29.5 4.1 %shard_map.161 = f32[2,32,128]{2,1,0:T(8,128)S(1)} custom-call(f32[32,4,512]{2,1,0:T(4,128)S(1)} %all-to-all-done.refs_0_, f32[32,128]{1,0:T(8,128)S(1)} %bitcast.39, f32[32,128]{1,0:T(8,128)S(1)} %bitcast.40), custom_call_target="tpu_custom_call" | custom-call | tf_op jit(solution)/shard_map/pallas_call | solution.py:279
  33.6 0.1 collective-permute-start.5
  33.7 0.0 copy-start.5
  33.7 3.7 %collective-permute-start.2 = (f32[8,128]{1,0:T(8,128)S(1)}, f32[8,128]{1,0:T(8,128)S(1)}, u32[]{:S(2)}, u32[]{:S(2)}) collective-permute-start(f32[8,128]{1,0:T(8,128)S(1)} %get-tuple-element.14), channel_id=1, source_target_pairs={{0,248},{8,0},{16,8},{24,16},{32,24},{40,32},{48,40},{56,48},{64,5... | collective-permute-start | bytes 12296 | tf_op jit(solution)/shard_map/ppermute | solution.py:345
  37.5 1.3 %collective-permute-done.2.refs_9_ = f32[8,128]{1,0:T(8,128)S(1)} collective-permute-done((f32[8,128]{1,0:T(8,128)S(1)}, f32[8,128]{1,0:T(8,128)S(1)}, u32[]{:S(2)}, u32[]{:S(2)}) %collective-permute-start.2) | collective-permute-done | bytes 4128 | tf_op jit(solution)/shard_map/ppermute | solution.py:345
  38.8 1.7 %shard_map.159 = (f32[4,2,32,128]{3,2,1,0:T(8,128)S(1)}, f32[11,32,128]{2,1,0:T(8,128)S(1)}, f32[6,32,128]{2,1,0:T(8,128)S(1)}, f32[1,32,128]{2,1,0:T(8,128)S(1)}) custom-call(s32[32]{0:T(128)S(1)} %copy-done.9, f32[4,2,32,128]{3,2,1,0:T(8,128)S(1)} %bitcast.31, f32[2,32,128]{2,1,0:T(8,128)S(1)} %bitcast.19, f32[2,32,128]{2,1,0:T(8,128)S(1)} %bitcast.23, ...), custom_call_target="tpu_custom_call" | custom-call | tf_op jit(solution)/shard_map/pallas_call | solution.py:279
  40.6 0.5 collective-permute-start.6
  41.1 3.7 %collective-permute-done.6 = f32[3,32,128]{2,1,0:T(8,128)S(1)} collective-permute-done((f32[3,32,128]{2,1,0:T(8,128)S(1)}, f32[3,32,128]{2,1,0:T(8,128)S(1)}, u32[]{:S(2)}, u32[]{:S(2)}) %collective-permute-start.6) | collective-permute-done | bytes 49184 | tf_op jit(solution)/shard_map/ppermute | solution.py:358
  44.8 4.4 %collective-permute-start.7 = (f32[3,32,128]{2,1,0:T(8,128)S(1)}, f32[3,32,128]{2,1,0:T(8,128)S(1)}, u32[]{:S(2)}, u32[]{:S(2)}) collective-permute-start(f32[3,32,128]{2,1,0:T(8,128)S(1)} %fusion.refs_2_), channel_id=1, source_target_pairs={{0,1},{1,0},{2,3},{3,2},{4,5},{5,4},{6,7},{7,6},{8,9},{9,8},{10,11... | collective-permute-start | bytes 147464 | tf_op jit(solution)/shard_map/ppermute | solution.py:360
  49.2 5.8 %collective-permute-start.10 = (f32[6,32,128]{2,1,0:T(8,128)S(1)}, f32[6,32,128]{2,1,0:T(8,128)S(1)}, u32[]{:S(2)}, u32[]{:S(2)}) collective-permute-start(f32[6,32,128]{2,1,0:T(8,128)S(1)} %get-tuple-element.19), channel_id=1, source_target_pairs={{1,2},{3,4},{5,6},{2,1},{4,3},{6,5},{9,10},{11,12},{13,14},{10,9},... | collective-permute-start | bytes 294920 | tf_op jit(solution)/shard_map/ppermute | solution.py:361
  55.0 0.0 copy-start.6
  55.0 1.6 %collective-permute-start.9 = (f32[11,32,128]{2,1,0:T(8,128)S(1)}, f32[11,32,128]{2,1,0:T(8,128)S(1)}, u32[]{:S(2)}, u32[]{:S(2)}) collective-permute-start(f32[11,32,128]{2,1,0:T(8,128)S(1)} %get-tuple-element.18), channel_id=1, source_target_pairs={{0,1},{1,0},{2,3},{3,2},{4,5},{5,4},{6,7},{7,6},{8,9},{9,8},{10,11... | collective-permute-start | bytes 540680 | tf_op jit(solution)/shard_map/ppermute | solution.py:359
  56.6 2.1 %collective-permute-start.8 = (f32[1,32,128]{2,1,0:T(8,128)S(1)}, f32[1,32,128]{2,1,0:T(8,128)S(1)}, u32[]{:S(2)}, u32[]{:S(2)}) collective-permute-start(f32[1,32,128]{2,1,0:T(8,128)S(1)} %slice_add_fusion.refs_5_), channel_id=1, source_target_pairs={{0,2},{1,3},{2,0},{3,1},{4,6},{5,7},{6,4},{7,5},{8,10},{9,11},{10,... | collective-permute-start | bytes 49160 | tf_op jit(solution)/shard_map/ppermute | solution.py:363
  58.7 9.9 %collective-permute-done.9.refs_5_.refs_12_ = f32[11,32,128]{2,1,0:T(8,128)S(1)} collective-permute-done((f32[11,32,128]{2,1,0:T(8,128)S(1)}, f32[11,32,128]{2,1,0:T(8,128)S(1)}, u32[]{:S(2)}, u32[]{:S(2)}) %collective-permute-start.9) | collective-permute-done | bytes 180256 | tf_op jit(solution)/shard_map/ppermute | solution.py:359
  68.6 1.6 %shard_map.162 = f32[8,128]{1,0:T(8,128)S(1)} custom-call(s32[32]{0:T(128)S(1)} %copy-done.9, f32[4,2,32,128]{3,2,1,0:T(8,128)S(1)} %get-tuple-element.16.refs_1_, f32[3,32,128]{2,1,0:T(8,128)S(1)} %fusion.refs_2_, f32[3,32,128]{2,1,0:T(8,128)S(1)} %collective-permute-done.7.refs_3_, f32[5,32,128]{2,1,0:T(8,128)S(1)} %add.16.refs_10_.refs_4_, ...), custom_call_target="tpu_custom_call" | custom-call | tf_op jit(solution)/shard_map/pallas_call | solution.py:279
  70.2 3.6 %collective-permute-start.11 = (f32[8,128]{1,0:T(8,128)S(1)}, f32[8,128]{1,0:T(8,128)S(1)}, u32[]{:S(2)}, u32[]{:S(2)}) collective-permute-start(f32[8,128]{1,0:T(8,128)S(1)} %shard_map.162), channel_id=1, source_target_pairs={{0,248},{8,0},{16,8},{24,16},{32,24},{40,32},{48,40},{56,48},{64,5... | collective-permute-start | bytes 12296 | tf_op jit(solution)/shard_map/ppermute | solution.py:368
  73.8 1.3 %collective-permute-done.11.refs_16_ = f32[8,128]{1,0:T(8,128)S(1)} collective-permute-done((f32[8,128]{1,0:T(8,128)S(1)}, f32[8,128]{1,0:T(8,128)S(1)}, u32[]{:S(2)}, u32[]{:S(2)}) %collective-permute-start.11) | collective-permute-done | bytes 4128 | tf_op jit(solution)/shard_map/ppermute | solution.py:368
  75.1 2.9 %shard_map.163 = (f32[4,2,32,128]{3,2,1,0:T(8,128)}, f32[32,128]{1,0:T(8,128)}) custom-call(s32[32]{0:T(128)S(1)} %copy-done.9, f32[4,2,32,128]{3,2,1,0:T(8,128)S(1)} %get-tuple-element.16.refs_1_, f32[3,32,128]{2,1,0:T(8,128)S(1)} %fusion.refs_2_, f32[3,32,128]{2,1,0:T(8,128)S(1)} %collective-permute-done.7.refs_3_, ...), custom_call_target="tpu_custom_call" | custom-call | tf_op jit(solution)/shard_map/pallas_call | solution.py:279
  (26 shorter events, 0.1 us)
Async XLA Ops:
  3.1 9.1 %copy-start = (f32[2,1,32,128]{3,2,1,0:T(8,128)S(1)}, f32[2,1,32,128]{3,2,1,0:T(8,128)}, u32[]{:S(2)}) copy-start(f32[2,1,32,128]{3,2,1,0:T(8,128)} %param.17) | copy-start | bytes 98308
  3.1 9.1 %copy-start.1 = (f32[2,1,32,128]{3,2,1,0:T(8,128)S(1)}, f32[2,1,32,128]{3,2,1,0:T(8,128)}, u32[]{:S(2)}) copy-start(f32[2,1,32,128]{3,2,1,0:T(8,128)} %param.19) | copy-start | bytes 98308
  3.1 9.1 %copy-start.2 = (f32[2,1,32,128]{3,2,1,0:T(8,128)S(1)}, f32[2,1,32,128]{3,2,1,0:T(8,128)}, u32[]{:S(2)}) copy-start(f32[2,1,32,128]{3,2,1,0:T(8,128)} %param.21) | copy-start | bytes 98308
  3.1 9.1 %copy-start.3 = (f32[4,2,1,32,128]{4,3,2,1,0:T(8,128)S(1)}, f32[4,2,1,32,128]{4,3,2,1,0:T(8,128)}, u32[]{:S(2)}) copy-start(f32[4,2,1,32,128]{4,3,2,1,0:T(8,128)} %param.15) | copy-start | bytes 393220
  3.1 9.1 %copy-start.4 = (f32[4,2,1,32,128]{4,3,2,1,0:T(8,128)S(1)}, f32[4,2,1,32,128]{4,3,2,1,0:T(8,128)}, u32[]{:S(2)}) copy-start(f32[4,2,1,32,128]{4,3,2,1,0:T(8,128)} %param.20) | copy-start | bytes 393220
  3.2 26.3 %all-to-all-start = ((f32[32,4,512]{2,1,0:T(4,128)}), f32[32,4,512]{2,1,0:T(4,128)S(1)}, u32[]{:S(2)}, u32[]{:S(2)}) async-start(f32[32,4,512]{2,1,0:T(4,128)} %shard_map.160), calls=%async_computation | async-start | bytes 524288 | tf_op jit(solution)/shard_map/all_to_all | solution.py:336
  12.2 0.7 copy-start.9
  14.1 4.7 %collective-permute-start.3 = (f32[5,32,128]{2,1,0:T(8,128)S(1)}, f32[5,32,128]{2,1,0:T(8,128)S(1)}, u32[]{:S(2)}, u32[]{:S(2)}) collective-permute-start(f32[5,32,128]{2,1,0:T(8,128)S(1)} %get-tuple-element.15), channel_id=1, source_target_pairs={{0,2},{1,3},{2,0},{3,1},{4,6},{5,7},{6,4},{7,5},{8,10},{9,11},{10,... | collective-permute-start | bytes 245768 | tf_op jit(solution)/shard_map/ppermute | solution.py:342
  18.8 10.7 %copy-start.7 = (f32[1,32,128]{2,1,0:T(8,128)S(1)}, f32[1,32,128]{2,1,0:T(8,128)}, u32[]{:S(2)}) copy-start(f32[1,32,128]{2,1,0:T(8,128)} %param.23) | copy-start | bytes 49156
  18.8 10.7 %copy-start.8 = (f32[1,32,128]{2,1,0:T(8,128)S(1)}, f32[1,32,128]{2,1,0:T(8,128)}, u32[]{:S(2)}) copy-start(f32[1,32,128]{2,1,0:T(8,128)} %param.24) | copy-start | bytes 49156
  18.8 18.7 %collective-permute-start.4 = (f32[5,32,128]{2,1,0:T(8,128)S(1)}, f32[5,32,128]{2,1,0:T(8,128)S(1)}, u32[]{:S(2)}, u32[]{:S(2)}) collective-permute-start(f32[5,32,128]{2,1,0:T(8,128)S(1)} %add.15), channel_id=1, source_target_pairs={{0,6},{1,7},{2,4},{3,5},{4,2},{5,3},{6,0},{7,1},{8,14},{9,15},{10,... | collective-permute-start | bytes 245768 | tf_op jit(solution)/shard_map/ppermute | solution.py:346
  20.4 18.4 %collective-permute-start = (f32[5,32,128]{2,1,0:T(8,128)S(1)}, f32[5,32,128]{2,1,0:T(8,128)S(1)}, u32[]{:S(2)}, u32[]{:S(2)}) collective-permute-start(f32[5,32,128]{2,1,0:T(8,128)S(1)} %get-tuple-element.12), channel_id=1, source_target_pairs={{0,1},{1,0},{2,3},{3,2},{4,5},{5,4},{6,7},{7,6},{8,9},{9,8},{10,11... | collective-permute-start | bytes 245768 | tf_op jit(solution)/shard_map/ppermute | solution.py:343
  24.9 13.9 %collective-permute-start.1 = (f32[5,32,128]{2,1,0:T(8,128)S(1)}, f32[5,32,128]{2,1,0:T(8,128)S(1)}, u32[]{:S(2)}, u32[]{:S(2)}) collective-permute-start(f32[5,32,128]{2,1,0:T(8,128)S(1)} %get-tuple-element.13), channel_id=1, source_target_pairs={{1,2},{3,4},{5,6},{2,1},{4,3},{6,5},{9,10},{11,12},{13,14},{10,9},... | collective-permute-start | bytes 245768 | tf_op jit(solution)/shard_map/ppermute | solution.py:344
  33.6 6.9 %collective-permute-start.5 = (f32[2,32,128]{2,1,0:T(8,128)S(1)}, f32[2,32,128]{2,1,0:T(8,128)S(1)}, u32[]{:S(2)}, u32[]{:S(2)}) collective-permute-start(f32[2,32,128]{2,1,0:T(8,128)S(1)} %shard_map.161), channel_id=1, source_target_pairs={{0,2},{1,3},{2,0},{3,1},{4,6},{5,7},{6,4},{7,5},{8,10},{9,11},{10,... | collective-permute-start | bytes 98312 | tf_op jit(solution)/shard_map/ppermute | solution.py:351
  33.7 5.1 %copy-start.5 = (f32[1,32,128]{2,1,0:T(8,128)S(1)}, f32[1,32,128]{2,1,0:T(8,128)}, u32[]{:S(2)}) copy-start(f32[1,32,128]{2,1,0:T(8,128)} %param.18) | copy-start | bytes 49156
  33.7 5.1 %collective-permute-start.2 = (f32[8,128]{1,0:T(8,128)S(1)}, f32[8,128]{1,0:T(8,128)S(1)}, u32[]{:S(2)}, u32[]{:S(2)}) collective-permute-start(f32[8,128]{1,0:T(8,128)S(1)} %get-tuple-element.14), channel_id=1, source_target_pairs={{0,248},{8,0},{16,8},{24,16},{32,24},{40,32},{48,40},{56,48},{64,5... | collective-permute-start | bytes 12296 | tf_op jit(solution)/shard_map/ppermute | solution.py:345
  40.6 4.2 %collective-permute-start.6 = (f32[3,32,128]{2,1,0:T(8,128)S(1)}, f32[3,32,128]{2,1,0:T(8,128)S(1)}, u32[]{:S(2)}, u32[]{:S(2)}) collective-permute-start(f32[3,32,128]{2,1,0:T(8,128)S(1)} %pad_maximum_fusion), channel_id=1, source_target_pairs={{0,6},{1,7},{2,4},{3,5},{4,2},{5,3},{6,0},{7,1},{8,14},{9,15},{10,... | collective-permute-start | bytes 147464 | tf_op jit(solution)/shard_map/ppermute | solution.py:358
  44.8 11.8 %collective-permute-start.7 = (f32[3,32,128]{2,1,0:T(8,128)S(1)}, f32[3,32,128]{2,1,0:T(8,128)S(1)}, u32[]{:S(2)}, u32[]{:S(2)}) collective-permute-start(f32[3,32,128]{2,1,0:T(8,128)S(1)} %fusion.refs_2_), channel_id=1, source_target_pairs={{0,1},{1,0},{2,3},{3,2},{4,5},{5,4},{6,7},{7,6},{8,9},{9,8},{10,11... | collective-permute-start | bytes 147464 | tf_op jit(solution)/shard_map/ppermute | solution.py:360
  49.2 24.6 %collective-permute-start.10 = (f32[6,32,128]{2,1,0:T(8,128)S(1)}, f32[6,32,128]{2,1,0:T(8,128)S(1)}, u32[]{:S(2)}, u32[]{:S(2)}) collective-permute-start(f32[6,32,128]{2,1,0:T(8,128)S(1)} %get-tuple-element.19), channel_id=1, source_target_pairs={{1,2},{3,4},{5,6},{2,1},{4,3},{6,5},{9,10},{11,12},{13,14},{10,9},... | collective-permute-start | bytes 294920 | tf_op jit(solution)/shard_map/ppermute | solution.py:361
  55.0 13.6 %copy-start.6 = (f32[1,32,128]{2,1,0:T(8,128)S(1)}, f32[1,32,128]{2,1,0:T(8,128)}, u32[]{:S(2)}) copy-start(f32[1,32,128]{2,1,0:T(8,128)} %param.16) | copy-start | bytes 49156
  55.0 13.5 %collective-permute-start.9 = (f32[11,32,128]{2,1,0:T(8,128)S(1)}, f32[11,32,128]{2,1,0:T(8,128)S(1)}, u32[]{:S(2)}, u32[]{:S(2)}) collective-permute-start(f32[11,32,128]{2,1,0:T(8,128)S(1)} %get-tuple-element.18), channel_id=1, source_target_pairs={{0,1},{1,0},{2,3},{3,2},{4,5},{5,4},{6,7},{7,6},{8,9},{9,8},{10,11... | collective-permute-start | bytes 540680 | tf_op jit(solution)/shard_map/ppermute | solution.py:359
  56.6 18.5 %collective-permute-start.8 = (f32[1,32,128]{2,1,0:T(8,128)S(1)}, f32[1,32,128]{2,1,0:T(8,128)S(1)}, u32[]{:S(2)}, u32[]{:S(2)}) collective-permute-start(f32[1,32,128]{2,1,0:T(8,128)S(1)} %slice_add_fusion.refs_5_), channel_id=1, source_target_pairs={{0,2},{1,3},{2,0},{3,1},{4,6},{5,7},{6,4},{7,5},{8,10},{9,11},{10,... | collective-permute-start | bytes 49160 | tf_op jit(solution)/shard_map/ppermute | solution.py:363
  70.2 5.0 %collective-permute-start.11 = (f32[8,128]{1,0:T(8,128)S(1)}, f32[8,128]{1,0:T(8,128)S(1)}, u32[]{:S(2)}, u32[]{:S(2)}) collective-permute-start(f32[8,128]{1,0:T(8,128)S(1)} %shard_map.162), channel_id=1, source_target_pairs={{0,248},{8,0},{16,8},{24,16},{32,24},{40,32},{48,40},{56,48},{64,5... | collective-permute-start | bytes 12296 | tf_op jit(solution)/shard_map/ppermute | solution.py:368

commit v4 on v3

--- a/solution.py
+++ b/solution.py
@@ -8,32 +8,33 @@
 FIELDS = 4
 LEVELS_HERE = 2
 PIECES = 3
-ROWS_AT_ONCE = 8
+ROWS_AT_ONCE = 32
 MAP_HEIGHT, MAP_THERMAL, STEP_TWO = range(3)
 STEP_ONE, WEIGHTED, FLOW_TOP, STRETCH_TOP, THERMAL_GAIN = range(5)
-EARLY = 5
-HALO, MIDDLE = FIELDS + 1, FIELDS + 2
-
-
-def maps_kernel(records, thermal, elevation, out, total):
+LATE, EARLY = 3, 5
+MIX, HALO = FIELDS, FIELDS + 1
+WEIGHT, AFTER = FIELDS, FIELDS + 1
+MIDDLE = 2 * AFTER + 1
+
+
+def maps_kernel(records, thermal, elevation, ending, out, total):
     rows, cols = thermal.shape
-    sources, _, slots = records.shape
+    sources, slots = records.shape[0], records.shape[2] - cols
     half = jnp.bfloat16
-    row_of = lax.broadcasted_iota(jnp.int32, (2 * rows, slots), 0).astype(jnp.float32).astype(half)
-    col_of = lax.broadcasted_iota(jnp.int32, (cols, slots), 0).astype(jnp.float32).astype(half)
-    nothing = jnp.zeros((2 * rows, slots), half)
-    one, zero = jnp.ones((cols, slots), half), jnp.zeros((cols, slots), half)
+    row_of = lax.broadcasted_iota(jnp.int32, (rows, slots), 0).astype(jnp.float32).astype(half)
+    col_of = lax.broadcasted_iota(jnp.int32, (2 * cols, slots), 0).astype(jnp.float32).astype(half)
+    nothing = jnp.zeros((rows, slots), half)
+    one, zero = jnp.ones((2 * cols, slots), half), jnp.zeros((2 * cols, slots), half)
     total[...] = jnp.zeros_like(total)
 
     def body(i, carry):
         left, right = [], []
         for j in range(ROWS_AT_ONCE):
             weight, scaled, kind, place = (
-                records[i * ROWS_AT_ONCE + j, n : n + 1, :] for n in range(4)
+                records[i * ROWS_AT_ONCE + j, n : n + 1, :slots] for n in range(4)
             )
             row = jnp.floor(place * (1.0 / cols))
-            col = place - row * cols
-            row = row + kind * rows
+            col = place - row * cols + kind * cols
             here = jnp.broadcast_to(row.astype(half), nothing.shape) == row_of
             parts = []
             for rest in (weight, scaled):
@@ -52,17 +53,20 @@
         return carry
 
     lax.fori_loop(0, sources // ROWS_AT_ONCE, body, 0)
-    step = 2 * rows
-    weights = sum(total[n * step : (n + 1) * step] for n in range(PIECES))
-    values = sum(total[n * step : (n + 1) * step] for n in range(PIECES, 2 * PIECES))
-    out[MAP_THERMAL] = thermal[...] * weights[:rows] - values[:rows]
-    out[MAP_HEIGHT] = elevation[...] * weights[rows:] - values[rows:]
+    weights = sum(total[n * rows : (n + 1) * rows] for n in range(PIECES))
+    values = sum(total[n * rows : (n + 1) * rows] for n in range(PIECES, 2 * PIECES))
+    out[MAP_THERMAL] = thermal[...] * weights[:, :cols] - values[:, :cols]
+    height = elevation[...] * weights[:, cols:] - values[:, cols:]
+    out[MAP_HEIGHT] = jnp.where(lax.axis_index("lev") == 0, height + ending[...], height)
+
+
+def level_place():
+    lev = lax.axis_index("lev")
+    return lev, lev == lax.axis_size("lev") - 1, lev % 2 == 0
 
 
 def place(turned_ref):
-    lev = lax.axis_index("lev")
-    turned = turned_ref[lax.axis_index("tile")] == 1
-    return lev, lev == lax.axis_size("lev") - 1, lev % 2 == 0, turned
+    return *level_place(), turned_ref[lax.axis_index("tile")] == 1
 
 
 def along_columns(value, last):
@@ -116,19 +120,23 @@
     out[...] = jnp.concatenate([*lines, rest], 0)
 
 
-def packet_kernel(counts, measured, precision, kind, location, packet):
+def packet_kernel(turned_ref, counts, state, flow, measured, precision, kind, location, packet):
+    _, _, _, turned = place(turned_ref)
     sources, slots = measured.shape
     lane = lax.broadcasted_iota(jnp.int32, (1, slots), 1)
+    lines = edges([[state[f, k] for k in range(LEVELS_HERE)] for f in range(FIELDS)], [flow[0], flow[1]], turned)
+    block = jnp.concatenate(lines, 0)
     for s in range(sources):
         weight = jnp.where(lane < counts[s], precision[s : s + 1, :], 0.0)
-        packet[s, 0:1, :] = weight
-        packet[s, 1:2, :] = weight * measured[s : s + 1, :]
-        packet[s, 2:3, :] = kind[s : s + 1, :].astype(jnp.float32)
-        packet[s, 3:4, :] = location[s : s + 1, :].astype(jnp.float32)
-
-
-def start_kernel(turned_ref, state, flow, mix, stretch, weight, to_flip, to_other, early, edge):
-    lev, _, low, turned = place(turned_ref)
+        packet[s, 0:1, :slots] = weight
+        packet[s, 1:2, :slots] = weight * measured[s : s + 1, :]
+        packet[s, 2:3, :slots] = kind[s : s + 1, :].astype(jnp.float32)
+        packet[s, 3:4, :slots] = location[s : s + 1, :].astype(jnp.float32)
+        packet[s, :, slots:] = block
+
+
+def start_kernel(state, flow, mix, stretch, weight, to_flip, to_other, early):
+    lev, _, low = level_place()
     first = lev == 0
     column = None
     for f in range(FIELDS):
@@ -137,8 +145,8 @@
         to_other[f] = jnp.where(low, top, bottom)
         term = stretch[f, 0] * top + stretch[f, 1] * bottom
         column = term if column is None else column + term
-    to_flip[FIELDS] = mix[1]
-    to_other[FIELDS] = mix[1]
+    to_flip[MIX] = mix[1]
+    to_other[MIX] = mix[1]
     none = jnp.zeros_like(column)
     gain = stretch[0, 0] * (1.0 - flow[0] - mix[0]) + stretch[0, 1] * mix[0]
     early[STEP_ONE] = column
@@ -146,9 +154,6 @@
     early[FLOW_TOP] = jnp.where(first, flow[0], none)
     early[STRETCH_TOP] = jnp.where(first, stretch[0, 0], none)
     early[THERMAL_GAIN] = jnp.where(first, gain, none)
-    store_lines(
-        edges([[state[f, k] for k in range(LEVELS_HERE)] for f in range(FIELDS)], [flow[0], flow[1]], turned), edge
-    )
 
 
 def step(fields, flow, mix, mix_low, mix_high, spread_y, lines, above, below):
@@ -163,31 +168,25 @@
         yield f, new_top, new_bottom
 
 
-def step_one_kernel(
-    turned_ref, state, flow, mix, stretch, spread, weight, flipped, crossed, edge, early,
-    own, to_flip, to_other, column_out,
-):
-    _, last, low, _ = place(turned_ref)
+def step_one_kernel(state, flow, mix, stretch, weight, spread, halo, edge, own, packed, column_out):
+    _, last, low = level_place()
     mix_low = jnp.where(last, 0.0, mix[1])
-    mix_high = jnp.where(low, crossed[FIELDS], flipped[FIELDS])
+    mix_high = jnp.where(low, halo[HALO + MIX], halo[MIX])
     column = None
     for f, top, bottom in step(
         lambda f: (state[f, 0], state[f, 1]), flow, mix, mix_low, mix_high, masked_spread(spread), edge,
-        lambda f: jnp.where(low, crossed[f], flipped[f]),
-        lambda f: jnp.where(low, flipped[f], crossed[f]),
+        lambda f: jnp.where(low, halo[HALO + f], halo[f]),
+        lambda f: jnp.where(low, halo[f], halo[HALO + f]),
     ):
         own[f, 0] = top
         own[f, 1] = bottom
-        to_flip[f] = jnp.where(low, bottom, top)
-        to_other[f] = jnp.where(low, top, bottom)
+        packed[f] = jnp.where(low, bottom, top)
+        packed[AFTER + f] = jnp.where(low, top, bottom)
         term = stretch[f, 0] * top + stretch[f, 1] * bottom
         column = term if column is None else column + term
-    to_flip[FIELDS] = jnp.where(low, weight[1], weight[0])
-    to_other[FIELDS] = jnp.where(low, weight[0], weight[1])
-    to_flip[FIELDS + 1] = mix[0]
-    to_other[FIELDS + 1] = mix[0]
-    for n in range(EARLY):
-        to_flip[MIDDLE + n] = early[n]
+    packed[WEIGHT] = jnp.where(low, weight[1], weight[0])
+    packed[AFTER + WEIGHT] = jnp.where(low, weight[0], weight[1])
+    packed[2 * AFTER] = mix[0]
     column_out[0] = column
 
 
@@ -201,12 +200,12 @@
     return fields
 
 
-def edge_kernel(turned_ref, own, half, other, early, flipped, elevation, flow, mix, spread, weight, edge):
+def edge_kernel(turned_ref, own, half, other, flow, mix, spread, weight, edge):
     lev, _, _, turned = place(turned_ref)
     rows = spread.shape[0]
-    height = elevation[...] + (half[MAP_HEIGHT] + other[MAP_HEIGHT])
+    height = half[MAP_HEIGHT] + other[MAP_HEIGHT]
     thermal = half[MAP_THERMAL] + other[MAP_THERMAL]
-    flow_top = early[FLOW_TOP] + flipped[MIDDLE + FLOW_TOP]
+    flow_top = half[LATE + FLOW_TOP] + other[LATE + FLOW_TOP]
     fields = middle_state(
         lev == 0, own, thermal, height, flow, weight, mix, masked_spread(spread), jnp.zeros((rows, 1), jnp.float32)
     )
@@ -216,22 +215,22 @@
 
 
 def step_two_kernel(
-    turned_ref, own, half, other, early, column, column_other, elevation, flow, mix, spread, weight,
-    flipped, crossed, old_flipped, old_crossed, edge, out_state, out_height,
+    own, half, other, column, column_other, flow, mix, spread, weight,
+    flipped, crossed, halo, edge, out_state, out_height,
 ):
-    lev, last, low, _ = place(turned_ref)
+    lev, last, low = level_place()
     rows = spread.shape[0]
     spread_y = masked_spread(spread)
     mix_low = jnp.where(last, 0.0, mix[1])
-    mix_high = jnp.where(low, old_crossed[FIELDS], old_flipped[FIELDS])
-    weight_above = jnp.where(low, crossed[FIELDS], flipped[FIELDS])
-    weight_below = jnp.where(low, flipped[FIELDS], crossed[FIELDS])
+    mix_high = jnp.where(low, halo[HALO + MIX], halo[MIX])
+    weight_above = jnp.where(low, crossed[WEIGHT], flipped[WEIGHT])
+    weight_below = jnp.where(low, flipped[WEIGHT], crossed[WEIGHT])
 
     def total(n):
-        return early[n] + flipped[MIDDLE + n]
+        return half[LATE + n] + other[LATE + n]
 
     thermal = half[MAP_THERMAL] + other[MAP_THERMAL]
-    height = elevation[...] + (half[MAP_HEIGHT] + other[MAP_HEIGHT])
+    height = half[MAP_HEIGHT] + other[MAP_HEIGHT]
     stretch_top = total(STRETCH_TOP)
     seam = to_column(edge[FIELDS : FIELDS + 1, :], rows, 0)
     fields = middle_state(lev == 0, own, thermal, height, flow, weight, mix, spread_y, seam)
@@ -240,7 +239,7 @@
     def above(f):
         value = jnp.where(low, crossed[f], flipped[f])
         if f == 0:
-            value = value + jnp.where(lev == 1, flipped[FIELDS + 1] * thermal, 0.0)
+            value = value + jnp.where(lev == 1, flipped[2 * AFTER] * thermal, 0.0)
         return value + weight_above * height if f == 2 else value
 
     def below(f):
@@ -261,7 +260,8 @@
     )
 
 
-def call(kernel, operands, shapes, smem=(), scratch=(), grant=16 << 20):
+def call(kernel, operands, shapes, smem=(), scratch=(), grant=16 << 20, at=None):
+    at = at or {}
     count, outs = len(operands), len(shapes)
 
     def body(*refs):
@@ -269,6 +269,7 @@
         sources, refs = refs[:count], refs[count:]
         results, refs = refs[:outs], refs[outs:]
         held, semaphores, rest = refs[:count], refs[count], refs[count + 1 :]
+        sources = [at[n][1](s) if n in at else s for n, s in enumerate(sources)]
         copies = [pltpu.make_async_copy(s, h, semaphores.at[n]) for n, (s, h) in enumerate(zip(sources, held))]
         for copy in copies:
             copy.start()
@@ -282,7 +283,7 @@
         in_specs=[pl.BlockSpec(memory_space=pltpu.SMEM)] * len(smem) + [pl.BlockSpec(memory_space=pl.ANY)] * count,
         out_specs=[pl.BlockSpec(memory_space=pltpu.VMEM)] * outs,
         scratch_shapes=[
-            *(pltpu.VMEM(o.shape, o.dtype) for o in operands),
+            *(pltpu.VMEM(at[n][0] if n in at else o.shape, o.dtype) for n, o in enumerate(operands)),
             pltpu.SemaphoreType.DMA((count,)),
             *scratch,
         ],
@@ -313,7 +314,8 @@
     groups = lax.axis_size("lev")
     tiles = lax.axis_size("tile")
     flip = [(l, l ^ 1) for l in range(groups)]
-    cross = [(l, l + 1) for l in range(1, groups - 1, 2)] + [(l + 1, l) for l in range(1, groups - 1, 2)]
+    inward = [(l, l - 2) for l in range(2, groups, 2)] + [(l, l + 2) for l in range(1, groups - 2, 2)]
+    outward = [(destination, source) for source, destination in inward]
     pair = [(l, l ^ 2) for l in range(groups)]
     mirror = [(l, groups - 2 - (l & ~1) + (l & 1)) for l in range(groups)]
     west = [(t, (t - 1) % tiles) for t in range(tiles)]
@@ -330,47 +332,52 @@
     field = (rows, cols)
     (packet,) = call(
         packet_kernel,
-        (measured_quantity[0, 0], measurement_precision[0, 0], measurement_sort[0, 0], sampled_location[0, 0]),
-        [(tiles, 4, slots)], smem=(active_entry_numbers[0, 0],), grant=60 * 1024 * 1024,
+        (state, flow, measured_quantity[0, 0], measurement_precision[0, 0], measurement_sort[0, 0], sampled_location[0, 0]),
+        [(tiles, 4, slots + cols)], smem=(turned, active_entry_numbers[0, 0]), grant=60 * 1024 * 1024,
     )
     arrived = lax.all_to_all(packet, "tile", split_axis=0, concat_axis=0, tiled=True)
 
-    to_flip, to_other, early, edge = call(
+    to_flip, to_other, early = call(
         start_kernel, (state, flow, mix, stretch, weight),
-        [(HALO, *field), (HALO, *field), (EARLY, *field), (8, cols)], smem=(turned,),
-    )
+        [(HALO, *field), (HALO, *field), (EARLY, *field)],
+    )
+    relayed = lax.ppermute(to_other, "lev", inward)
     early = early + lax.ppermute(early, "lev", pair)
-    old_flipped = lax.ppermute(to_flip, "lev", flip)
-    old_crossed = lax.ppermute(to_other, "lev", cross)
+    halo = lax.ppermute(jnp.concatenate([to_flip, relayed]), "lev", flip)
+    (sums,) = call(
+        maps_kernel, (arrived, predicted_thermal_skin[0], predicted_elevation[0], elevation),
+        [(2, *field)], grant=24 << 20,
+        scratch=[pltpu.VMEM((2 * PIECES * rows, 2 * cols), jnp.float32)],
+    )
+    sums = sums + lax.ppermute(sums, "lev", pair)
+    own, packed, column = call(
+        step_one_kernel,
+        (state, flow, mix, stretch, weight, spread, halo, arrived),
+        [state.shape, (MIDDLE, *field), (1, *field)],
+        at={
+            7: (
+                (4, cols),
+                lambda ref: ref.at[lax.rem(lax.axis_index("tile") + 1, tiles), :, pl.ds(slots, cols)],
+            )
+        },
+    )
+    half = jnp.concatenate([sums, column, early])
+    half = half + lax.ppermute(half, "lev", mirror)
+    flipped = lax.ppermute(packed, "lev", flip)
+    other = lax.ppermute(half, "lev", flip)
+    (edge,) = call(
+        edge_kernel, (own, half, other, flow, mix, spread, weight),
+        [(8, cols)], smem=(turned,),
+    )
     edge = lax.ppermute(edge, "tile", west)
-    early = early + lax.ppermute(early, "lev", mirror)
-    (sums,) = call(
-        maps_kernel, (arrived, predicted_thermal_skin[0], predicted_elevation[0]),
-        [(2, *field)], scratch=[pltpu.VMEM((4 * PIECES * rows, cols), jnp.float32)],
-    )
-    sums = sums + lax.ppermute(sums, "lev", pair)
-    own, to_flip, to_other, column = call(
-        step_one_kernel,
-        (state, flow, mix, stretch, spread, weight, old_flipped, old_crossed, edge, early),
-        [state.shape, (MIDDLE + EARLY, *field), (MIDDLE, *field), (1, *field)], smem=(turned,),
-    )
-    both = jnp.concatenate([sums, column])
-    both = both + lax.ppermute(both, "lev", mirror)
-    flipped = lax.ppermute(to_flip, "lev", flip)
-    other = lax.ppermute(both, "lev", flip)
-    crossed = lax.ppermute(to_other, "lev", cross)
-    column = both[STEP_TWO:] + other[STEP_TWO:]
+    crossed = lax.ppermute(flipped[AFTER : 2 * AFTER], "lev", outward)
+    column = half[STEP_TWO:LATE] + other[STEP_TWO:LATE]
     column_other = lax.ppermute(column, "lev", pair)
-    (edge,) = call(
-        edge_kernel, (own, both, other, early, flipped, elevation, flow, mix, spread, weight),
-        [(8, cols)], smem=(turned,),
-    )
-    edge = lax.ppermute(edge, "tile", west)
     out_state, out_height = call(
         step_two_kernel,
-        (own, both, other, early, column, column_other, elevation, flow, mix, spread, weight,
-         flipped, crossed, old_flipped, old_crossed, edge),
-        [state.shape, field], smem=(turned,),
+        (own, half, other, column, column_other, flow, mix, spread, weight,
+         flipped, crossed, halo, edge),
+        [state.shape, field],
     )
     return (out_state[:, :, None], out_height[None])
 

time: 78.4 us -> 63.8 us (0.81)
  the two profiles are of different devices: /device:TPU:2 before, /device:TPU:57 now
where the time goes in v4:
time: 63.8 us; the launch traced here: 63.4 us
  starting transfers between devices  27.6 us (43%)
  waiting for transfers between devices  23 us (36%)
  Pallas kernels  11.1 us (17%)
  between operations  0.84 us (1%)
  local copies, waits for them, and re-layouts  0.7 us (1%)
    pallas_call x6, Pallas kernels, call(): pl.pallas_call(body, out_shape=[jax.ShapeDtypeStruct(shape, jnp.float32)...  11.1 us
    all_to_all x1, starting transfers between devices, per_device(): lax.all_to_all(packet, 'tile', split_axis=0, concat_axis=0, tiled=True)  8.88 us
    ppermute x1, waiting for transfers between devices, per_device(): flipped = lax.ppermute(packed, 'lev', flip)  8.63 us
    ppermute x1, starting transfers between devices, per_device(): half = half + lax.ppermute(half, 'lev', mirror)  4.6 us
    ppermute x1, waiting for transfers between devices, per_device(): relayed = lax.ppermute(to_other, 'lev', inward)  4.2 us
    ppermute x1, waiting for transfers between devices, per_device(): edge = lax.ppermute(edge, 'tile', west)  3.85 us
    ppermute x1, waiting for transfers between devices, per_device(): other = lax.ppermute(half, 'lev', flip)  3.51 us
    ppermute x1, starting transfers between devices, per_device(): halo = lax.ppermute(jnp.concatenate([to_flip, relayed]), 'lev', flip)  3.39 us
  transfers between devices with their start and end apart: 11, of which 7 were waited for; matrix products, arithmetic and copies ran while one was open for 0% of the time, Pallas kernels for 10%

profile of v4, /device:TPU:57, one launch (start us, length us, event | category | flops | bytes accessed | tf_op | source)
XLA Modules:
  0.0 63.4 jit_solution(16610999949154066049)
XLA Ops:
  0.6 2.6 %shard_map.159 = f32[32,4,640]{2,1,0:T(4,128)} custom-call(s32[32]{0:T(128)} %refs_0_.3, s32[32]{0:T(128)} %bitcast.46, f32[4,2,32,128]{3,2,1,0:T(8,128)} %bitcast.18, f32[2,32,128]{2,1,0:T(8,128)} %bitcast.21, f32[32,512]{1,0:T(8,128)} %bitcast.42, f32[32,512]{1,0:T(8,128)} %bitcast.43, s32[32,512]{1,0:T(8,128)} %bitcast.44, s32[32,512]{1,0:T(8,128)} %bitcast.45), custom_call_target="tpu_custom_call" | custom-call | tf_op jit(solution)/shard_map/pallas_call | solution.py:280
  3.3 0.0 copy-start
  3.3 0.0 copy-start.1
  3.3 0.0 copy-start.2
  3.3 0.0 copy-start.3
  3.3 0.0 copy-start.4
  3.3 8.9 %all-to-all-start = ((f32[32,4,640]{2,1,0:T(4,128)}), f32[32,4,640]{2,1,0:T(4,128)S(1)}, u32[]{:S(2)}, u32[]{:S(2)}) async-start(f32[32,4,640]{2,1,0:T(4,128)} %shard_map.159), calls=%async_computation | async-start | bytes 655360 | tf_op jit(solution)/shard_map/all_to_all | solution.py:338
  12.3 0.5 shard_map.158
  12.8 1.3 %collective-permute-start = (f32[5,32,128]{2,1,0:T(8,128)S(1)}, f32[5,32,128]{2,1,0:T(8,128)S(1)}, u32[]{:S(2)}, u32[]{:S(2)}) collective-permute-start(f32[5,32,128]{2,1,0:T(8,128)S(1)} %get-tuple-element.11), channel_id=1, source_target_pairs={{2,0},{4,2},{6,4},{1,3},{3,5},{5,7},{10,8},{12,10},{14,12},{9,11},... | collective-permute-start | bytes 245768 | tf_op jit(solution)/shard_map/ppermute | solution.py:344
  14.1 4.2 %collective-permute-done = f32[5,32,128]{2,1,0:T(8,128)S(1)} collective-permute-done((f32[5,32,128]{2,1,0:T(8,128)S(1)}, f32[5,32,128]{2,1,0:T(8,128)S(1)}, u32[]{:S(2)}, u32[]{:S(2)}) %collective-permute-start) | collective-permute-done | bytes 81952 | tf_op jit(solution)/shard_map/ppermute | solution.py:344
  18.4 3.4 %collective-permute-start.1 = (f32[10,32,128]{2,1,0:T(8,128)S(1)}, f32[10,32,128]{2,1,0:T(8,128)S(1)}, u32[]{:S(2)}, u32[]{:S(2)}) collective-permute-start(f32[10,32,128]{2,1,0:T(8,128)S(1)} %pad_maximum_fusion), channel_id=1, source_target_pairs={{0,1},{1,0},{2,3},{3,2},{4,5},{5,4},{6,7},{7,6},{8,9},{9,8},{10,11... | collective-permute-start | bytes 491528 | tf_op jit(solution)/shard_map/ppermute | solution.py:346
  21.7 2.1 %collective-permute-start.3 = (f32[5,32,128]{2,1,0:T(8,128)S(1)}, f32[5,32,128]{2,1,0:T(8,128)S(1)}, u32[]{:S(2)}, u32[]{:S(2)}) collective-permute-start(f32[5,32,128]{2,1,0:T(8,128)S(1)} %get-tuple-element.14), channel_id=1, source_target_pairs={{0,2},{1,3},{2,0},{3,1},{4,6},{5,7},{6,4},{7,5},{8,10},{9,11},{10,... | collective-permute-start | bytes 245768 | tf_op jit(solution)/shard_map/ppermute | solution.py:345
  23.9 0.0 all-to-all-done.refs_7_.refs_0_
  23.9 3.1 %shard_map.161 = f32[2,32,128]{2,1,0:T(8,128)S(1)} custom-call(f32[32,4,640]{2,1,0:T(4,128)S(1)} %all-to-all-done.refs_7_.refs_0_, f32[32,128]{1,0:T(8,128)S(1)} %bitcast.39, f32[32,128]{1,0:T(8,128)S(1)} %bitcast.40, f32[32,128]{1,0:T(8,128)S(1)} %bitcast.41), custom_call_target="tpu_custom_call" | custom-call | tf_op jit(solution)/shard_map/pallas_call | solution.py:280
  27.0 0.0 copy-start.5
  27.0 0.1 collective-permute-start.2
  27.1 0.0 collective-permute-done.3
  27.2 1.6 %collective-permute-done.1.refs_6_.refs_11_ = f32[10,32,128]{2,1,0:T(8,128)S(1)} collective-permute-done((f32[10,32,128]{2,1,0:T(8,128)S(1)}, f32[10,32,128]{2,1,0:T(8,128)S(1)}, u32[]{:S(2)}, u32[]{:S(2)}) %collective-permute-start.1) | collective-permute-done | bytes 163872 | tf_op jit(solution)/shard_map/ppermute | solution.py:346
  28.8 1.0 %shard_map.160 = (f32[4,2,32,128]{3,2,1,0:T(8,128)S(1)}, f32[11,32,128]{2,1,0:T(8,128)S(1)}, f32[1,32,128]{2,1,0:T(8,128)S(1)}) custom-call(f32[4,2,32,128]{3,2,1,0:T(8,128)S(1)} %bitcast.20, f32[2,32,128]{2,1,0:T(8,128)S(1)} %bitcast.23, f32[2,32,128]{2,1,0:T(8,128)S(1)} %bitcast.29, f32[4,2,32,128]{3,2,1,0:T(8,128)S(1)} %bitcast.27, ...), custom_call_target="tpu_custom_call" | custom-call | tf_op jit(solution)/shard_map/pallas_call | solution.py:280
  29.8 0.3 collective-permute-done.2
  30.2 4.6 %collective-permute-start.4 = (f32[8,32,128]{2,1,0:T(8,128)S(1)}, f32[8,32,128]{2,1,0:T(8,128)S(1)}, u32[]{:S(2)}, u32[]{:S(2)}) collective-permute-start(f32[8,32,128]{2,1,0:T(8,128)S(1)} %pad_maximum_fusion.1), channel_id=1, source_target_pairs={{0,6},{1,7},{2,4},{3,5},{4,2},{5,3},{6,0},{7,1},{8,14},{9,15},{10,... | collective-permute-start | bytes 393224 | tf_op jit(solution)/shard_map/ppermute | solution.py:365
  34.8 1.5 %collective-permute-start.7 = (f32[11,32,128]{2,1,0:T(8,128)S(1)}, f32[11,32,128]{2,1,0:T(8,128)S(1)}, u32[]{:S(2)}, u32[]{:S(2)}) collective-permute-start(f32[11,32,128]{2,1,0:T(8,128)S(1)} %get-tuple-element.15), channel_id=1, source_target_pairs={{0,1},{1,0},{2,3},{3,2},{4,5},{5,4},{6,7},{7,6},{8,9},{9,8},{10,11... | collective-permute-start | bytes 540680 | tf_op jit(solution)/shard_map/ppermute | solution.py:366
  36.2 0.9 %collective-permute-done.4 = f32[8,32,128]{2,1,0:T(8,128)S(1)} collective-permute-done((f32[8,32,128]{2,1,0:T(8,128)S(1)}, f32[8,32,128]{2,1,0:T(8,128)S(1)}, u32[]{:S(2)}, u32[]{:S(2)}) %collective-permute-start.4) | collective-permute-done | bytes 131104 | tf_op jit(solution)/shard_map/ppermute | solution.py:365
  37.1 3.1 %collective-permute-start.5 = (f32[8,32,128]{2,1,0:T(8,128)S(1)}, f32[8,32,128]{2,1,0:T(8,128)S(1)}, u32[]{:S(2)}, u32[]{:S(2)}) collective-permute-start(f32[8,32,128]{2,1,0:T(8,128)S(1)} %fusion.refs_2_.refs_1_), channel_id=1, source_target_pairs={{0,1},{1,0},{2,3},{3,2},{4,5},{5,4},{6,7},{7,6},{8,9},{9,8},{10,11... | collective-permute-start | bytes 393224 | tf_op jit(solution)/shard_map/ppermute | solution.py:367
  40.3 8.6 %collective-permute-done.7.refs_9_ = f32[11,32,128]{2,1,0:T(8,128)S(1)} collective-permute-done((f32[11,32,128]{2,1,0:T(8,128)S(1)}, f32[11,32,128]{2,1,0:T(8,128)S(1)}, u32[]{:S(2)}, u32[]{:S(2)}) %collective-permute-start.7) | collective-permute-done | bytes 180256 | tf_op jit(solution)/shard_map/ppermute | solution.py:366
  48.9 1.3 %collective-permute-start.8 = (f32[5,32,128]{2,1,0:T(8,128)S(1)}, f32[5,32,128]{2,1,0:T(8,128)S(1)}, u32[]{:S(2)}, u32[]{:S(2)}) collective-permute-start(f32[5,32,128]{2,1,0:T(8,128)S(1)} %slice.14), channel_id=1, source_target_pairs={{0,2},{2,4},{4,6},{3,1},{5,3},{7,5},{8,10},{10,12},{12,14},{11,9},... | collective-permute-start | bytes 245768 | tf_op jit(solution)/shard_map/ppermute | solution.py:373
  50.2 3.5 %collective-permute-done.5.refs_3_.refs_2_ = f32[8,32,128]{2,1,0:T(8,128)S(1)} collective-permute-done((f32[8,32,128]{2,1,0:T(8,128)S(1)}, f32[8,32,128]{2,1,0:T(8,128)S(1)}, u32[]{:S(2)}, u32[]{:S(2)}) %collective-permute-start.5) | collective-permute-done | bytes 131104 | tf_op jit(solution)/shard_map/ppermute | solution.py:367
  53.7 0.6 %copy-done.9 = s32[32]{0:T(128)S(1)} copy-done((s32[32]{0:T(128)S(1)}, s32[32]{0:T(128)}, u32[]{:S(2)}) %copy-start.9) | copy-done | bytes 152
  54.4 1.4 %shard_map.162 = f32[8,128]{1,0:T(8,128)S(1)} custom-call(s32[32]{0:T(128)S(1)} %copy-done.9, f32[4,2,32,128]{3,2,1,0:T(8,128)S(1)} %get-tuple-element.12.refs_1_.refs_0_, f32[8,32,128]{2,1,0:T(8,128)S(1)} %fusion.refs_2_.refs_1_, f32[8,32,128]{2,1,0:T(8,128)S(1)} %collective-permute-done.5.refs_3_.refs_2_, f32[2,32,128]{2,1,0:T(8,128)S(1)} %bitcast.24, ...), custom_call_target="tpu_custom_call" | custom-call | tf_op jit(solution)/shard_map/pallas_call | solution.py:280
  55.8 1.4 %collective-permute-start.9 = (f32[8,128]{1,0:T(8,128)S(1)}, f32[8,128]{1,0:T(8,128)S(1)}, u32[]{:S(2)}, u32[]{:S(2)}) collective-permute-start(f32[8,128]{1,0:T(8,128)S(1)} %shard_map.162), channel_id=1, source_target_pairs={{0,248},{8,0},{16,8},{24,16},{32,24},{40,32},{48,40},{56,48},{64,5... | collective-permute-start | bytes 12296 | tf_op jit(solution)/shard_map/ppermute | solution.py:372
  57.2 3.8 %collective-permute-done.9.refs_12_ = f32[8,128]{1,0:T(8,128)S(1)} collective-permute-done((f32[8,128]{1,0:T(8,128)S(1)}, f32[8,128]{1,0:T(8,128)S(1)}, u32[]{:S(2)}, u32[]{:S(2)}) %collective-permute-start.9) | collective-permute-done | bytes 4128 | tf_op jit(solution)/shard_map/ppermute | solution.py:372
  61.0 2.4 %shard_map.163 = (f32[4,2,32,128]{3,2,1,0:T(8,128)}, f32[32,128]{1,0:T(8,128)}) custom-call(f32[4,2,32,128]{3,2,1,0:T(8,128)S(1)} %get-tuple-element.12.refs_1_.refs_0_, f32[8,32,128]{2,1,0:T(8,128)S(1)} %fusion.refs_2_.refs_1_, f32[8,32,128]{2,1,0:T(8,128)S(1)} %collective-permute-done.5.refs_3_.refs_2_, f32[1,32,128]{2,1,0:T(8,128)S(1)} %slice_add_fusion.refs_3_, ...), custom_call_target="tpu_custom_call" | custom-call | tf_op jit(solution)/shard_map/pallas_call | solution.py:280
  (23 shorter events, 0.1 us)
Async XLA Ops:
  3.3 9.0 %copy-start = (f32[4,2,1,32,128]{4,3,2,1,0:T(8,128)S(1)}, f32[4,2,1,32,128]{4,3,2,1,0:T(8,128)}, u32[]{:S(2)}) copy-start(f32[4,2,1,32,128]{4,3,2,1,0:T(8,128)} %param.15) | copy-start | bytes 393220
  3.3 9.0 %copy-start.1 = (f32[2,1,32,128]{3,2,1,0:T(8,128)S(1)}, f32[2,1,32,128]{3,2,1,0:T(8,128)}, u32[]{:S(2)}) copy-start(f32[2,1,32,128]{3,2,1,0:T(8,128)} %param.17) | copy-start | bytes 98308
  3.3 9.0 %copy-start.2 = (f32[4,2,1,32,128]{4,3,2,1,0:T(8,128)S(1)}, f32[4,2,1,32,128]{4,3,2,1,0:T(8,128)}, u32[]{:S(2)}) copy-start(f32[4,2,1,32,128]{4,3,2,1,0:T(8,128)} %param.20) | copy-start | bytes 393220
  3.3 8.9 %copy-start.3 = (f32[2,1,32,128]{3,2,1,0:T(8,128)S(1)}, f32[2,1,32,128]{3,2,1,0:T(8,128)}, u32[]{:S(2)}) copy-start(f32[2,1,32,128]{3,2,1,0:T(8,128)} %param.19) | copy-start | bytes 98308
  3.3 8.9 %copy-start.4 = (f32[2,1,32,128]{3,2,1,0:T(8,128)S(1)}, f32[2,1,32,128]{3,2,1,0:T(8,128)}, u32[]{:S(2)}) copy-start(f32[2,1,32,128]{3,2,1,0:T(8,128)} %param.21) | copy-start | bytes 98308
  3.3 20.5 %all-to-all-start = ((f32[32,4,640]{2,1,0:T(4,128)}), f32[32,4,640]{2,1,0:T(4,128)S(1)}, u32[]{:S(2)}, u32[]{:S(2)}) async-start(f32[32,4,640]{2,1,0:T(4,128)} %shard_map.159), calls=%async_computation | async-start | bytes 655360 | tf_op jit(solution)/shard_map/all_to_all | solution.py:338
  12.8 5.5 %collective-permute-start = (f32[5,32,128]{2,1,0:T(8,128)S(1)}, f32[5,32,128]{2,1,0:T(8,128)S(1)}, u32[]{:S(2)}, u32[]{:S(2)}) collective-permute-start(f32[5,32,128]{2,1,0:T(8,128)S(1)} %get-tuple-element.11), channel_id=1, source_target_pairs={{2,0},{4,2},{6,4},{1,3},{3,5},{5,7},{10,8},{12,10},{14,12},{9,11},... | collective-permute-start | bytes 245768 | tf_op jit(solution)/shard_map/ppermute | solution.py:344
  18.3 5.5 %copy-start.6 = (f32[1,32,128]{2,1,0:T(8,128)S(1)}, f32[1,32,128]{2,1,0:T(8,128)}, u32[]{:S(2)}) copy-start(f32[1,32,128]{2,1,0:T(8,128)} %param.23) | copy-start | bytes 49156
  18.3 5.5 %copy-start.7 = (f32[1,32,128]{2,1,0:T(8,128)S(1)}, f32[1,32,128]{2,1,0:T(8,128)}, u32[]{:S(2)}) copy-start(f32[1,32,128]{2,1,0:T(8,128)} %param.24) | copy-start | bytes 49156
  18.3 5.5 %copy-start.8 = (f32[1,32,128]{2,1,0:T(8,128)S(1)}, f32[1,32,128]{2,1,0:T(8,128)}, u32[]{:S(2)}) copy-start(f32[1,32,128]{2,1,0:T(8,128)} %param.16) | copy-start | bytes 49156
  18.4 10.4 %collective-permute-start.1 = (f32[10,32,128]{2,1,0:T(8,128)S(1)}, f32[10,32,128]{2,1,0:T(8,128)S(1)}, u32[]{:S(2)}, u32[]{:S(2)}) collective-permute-start(f32[10,32,128]{2,1,0:T(8,128)S(1)} %pad_maximum_fusion), channel_id=1, source_target_pairs={{0,1},{1,0},{2,3},{3,2},{4,5},{5,4},{6,7},{7,6},{8,9},{9,8},{10,11... | collective-permute-start | bytes 491528 | tf_op jit(solution)/shard_map/ppermute | solution.py:346
  21.7 5.4 %collective-permute-start.3 = (f32[5,32,128]{2,1,0:T(8,128)S(1)}, f32[5,32,128]{2,1,0:T(8,128)S(1)}, u32[]{:S(2)}, u32[]{:S(2)}) collective-permute-start(f32[5,32,128]{2,1,0:T(8,128)S(1)} %get-tuple-element.14), channel_id=1, source_target_pairs={{0,2},{1,3},{2,0},{3,1},{4,6},{5,7},{6,4},{7,5},{8,10},{9,11},{10,... | collective-permute-start | bytes 245768 | tf_op jit(solution)/shard_map/ppermute | solution.py:345
  27.0 1.8 %copy-start.5 = (f32[1,32,128]{2,1,0:T(8,128)S(1)}, f32[1,32,128]{2,1,0:T(8,128)}, u32[]{:S(2)}) copy-start(f32[1,32,128]{2,1,0:T(8,128)} %param.18) | copy-start | bytes 49156
  27.0 3.1 %collective-permute-start.2 = (f32[2,32,128]{2,1,0:T(8,128)S(1)}, f32[2,32,128]{2,1,0:T(8,128)S(1)}, u32[]{:S(2)}, u32[]{:S(2)}) collective-permute-start(f32[2,32,128]{2,1,0:T(8,128)S(1)} %shard_map.161), channel_id=1, source_target_pairs={{0,2},{1,3},{2,0},{3,1},{4,6},{5,7},{6,4},{7,5},{8,10},{9,11},{10,... | collective-permute-start | bytes 98312 | tf_op jit(solution)/shard_map/ppermute | solution.py:352
  30.2 7.0 %collective-permute-start.4 = (f32[8,32,128]{2,1,0:T(8,128)S(1)}, f32[8,32,128]{2,1,0:T(8,128)S(1)}, u32[]{:S(2)}, u32[]{:S(2)}) collective-permute-start(f32[8,32,128]{2,1,0:T(8,128)S(1)} %pad_maximum_fusion.1), channel_id=1, source_target_pairs={{0,6},{1,7},{2,4},{3,5},{4,2},{5,3},{6,0},{7,1},{8,14},{9,15},{10,... | collective-permute-start | bytes 393224 | tf_op jit(solution)/shard_map/ppermute | solution.py:365
  34.8 14.1 %collective-permute-start.7 = (f32[11,32,128]{2,1,0:T(8,128)S(1)}, f32[11,32,128]{2,1,0:T(8,128)S(1)}, u32[]{:S(2)}, u32[]{:S(2)}) collective-permute-start(f32[11,32,128]{2,1,0:T(8,128)S(1)} %get-tuple-element.15), channel_id=1, source_target_pairs={{0,1},{1,0},{2,3},{3,2},{4,5},{5,4},{6,7},{7,6},{8,9},{9,8},{10,11... | collective-permute-start | bytes 540680 | tf_op jit(solution)/shard_map/ppermute | solution.py:366
  37.1 16.6 %collective-permute-start.5 = (f32[8,32,128]{2,1,0:T(8,128)S(1)}, f32[8,32,128]{2,1,0:T(8,128)S(1)}, u32[]{:S(2)}, u32[]{:S(2)}) collective-permute-start(f32[8,32,128]{2,1,0:T(8,128)S(1)} %fusion.refs_2_.refs_1_), channel_id=1, source_target_pairs={{0,1},{1,0},{2,3},{3,2},{4,5},{5,4},{6,7},{7,6},{8,9},{9,8},{10,11... | collective-permute-start | bytes 393224 | tf_op jit(solution)/shard_map/ppermute | solution.py:367
  48.9 8.3 %collective-permute-start.8 = (f32[5,32,128]{2,1,0:T(8,128)S(1)}, f32[5,32,128]{2,1,0:T(8,128)S(1)}, u32[]{:S(2)}, u32[]{:S(2)}) collective-permute-start(f32[5,32,128]{2,1,0:T(8,128)S(1)} %slice.14), channel_id=1, source_target_pairs={{0,2},{2,4},{4,6},{3,1},{5,3},{7,5},{8,10},{10,12},{12,14},{11,9},... | collective-permute-start | bytes 245768 | tf_op jit(solution)/shard_map/ppermute | solution.py:373
  53.7 0.7 %copy-start.9 = (s32[32]{0:T(128)S(1)}, s32[32]{0:T(128)}, u32[]{:S(2)}) copy-start(s32[32]{0:T(128)} %refs_0_.3) | copy-start | bytes 388
  53.7 7.3 %collective-permute-start.6 = (f32[1,32,128]{2,1,0:T(8,128)S(1)}, f32[1,32,128]{2,1,0:T(8,128)S(1)}, u32[]{:S(2)}, u32[]{:S(2)}) collective-permute-start(f32[1,32,128]{2,1,0:T(8,128)S(1)} %slice_add_fusion.refs_3_), channel_id=1, source_target_pairs={{0,2},{1,3},{2,0},{3,1},{4,6},{5,7},{6,4},{7,5},{8,10},{9,11},{10,... | collective-permute-start | bytes 49160 | tf_op jit(solution)/shard_map/ppermute | solution.py:375
  55.8 5.2 %collective-permute-start.9 = (f32[8,128]{1,0:T(8,128)S(1)}, f32[8,128]{1,0:T(8,128)S(1)}, u32[]{:S(2)}, u32[]{:S(2)}) collective-permute-start(f32[8,128]{1,0:T(8,128)S(1)} %shard_map.162), channel_id=1, source_target_pairs={{0,248},{8,0},{16,8},{24,16},{32,24},{40,32},{48,40},{56,48},{64,5... | collective-permute-start | bytes 12296 | tf_op jit(solution)/shard_map/ppermute | solution.py:372

commit v5 on v4

--- a/solution.py
+++ b/solution.py
@@ -10,11 +10,11 @@
 PIECES = 3
 ROWS_AT_ONCE = 32
 MAP_HEIGHT, MAP_THERMAL, STEP_TWO = range(3)
-STEP_ONE, WEIGHTED, FLOW_TOP, STRETCH_TOP, THERMAL_GAIN = range(5)
+FLOW_TOP, STEP_ONE, WEIGHTED, STRETCH_TOP, THERMAL_GAIN = range(5)
 LATE, EARLY = 3, 5
+SOON = LATE + 1
 MIX, HALO = FIELDS, FIELDS + 1
-WEIGHT, AFTER = FIELDS, FIELDS + 1
-MIDDLE = 2 * AFTER + 1
+WEIGHT, UPPER, AFTER = FIELDS, FIELDS + 1, FIELDS + 2
 
 
 def maps_kernel(records, thermal, elevation, ending, out, total):
@@ -168,7 +168,7 @@
         yield f, new_top, new_bottom
 
 
-def step_one_kernel(state, flow, mix, stretch, weight, spread, halo, edge, own, packed, column_out):
+def step_one_kernel(state, flow, mix, stretch, weight, spread, halo, edge, own, to_flip, to_other, column_out):
     _, last, low = level_place()
     mix_low = jnp.where(last, 0.0, mix[1])
     mix_high = jnp.where(low, halo[HALO + MIX], halo[MIX])
@@ -180,13 +180,13 @@
     ):
         own[f, 0] = top
         own[f, 1] = bottom
-        packed[f] = jnp.where(low, bottom, top)
-        packed[AFTER + f] = jnp.where(low, top, bottom)
+        to_flip[f] = jnp.where(low, bottom, top)
+        to_other[f] = jnp.where(low, top, bottom)
         term = stretch[f, 0] * top + stretch[f, 1] * bottom
         column = term if column is None else column + term
-    packed[WEIGHT] = jnp.where(low, weight[1], weight[0])
-    packed[AFTER + WEIGHT] = jnp.where(low, weight[0], weight[1])
-    packed[2 * AFTER] = mix[0]
+    to_flip[WEIGHT] = jnp.where(low, weight[1], weight[0])
+    to_other[WEIGHT] = jnp.where(low, weight[0], weight[1])
+    to_flip[UPPER] = mix[0]
     column_out[0] = column
 
 
@@ -216,18 +216,18 @@
 
 def step_two_kernel(
     own, half, other, column, column_other, flow, mix, spread, weight,
-    flipped, crossed, halo, edge, out_state, out_height,
+    middle, halo, edge, out_state, out_height,
 ):
     lev, last, low = level_place()
     rows = spread.shape[0]
     spread_y = masked_spread(spread)
     mix_low = jnp.where(last, 0.0, mix[1])
     mix_high = jnp.where(low, halo[HALO + MIX], halo[MIX])
-    weight_above = jnp.where(low, crossed[WEIGHT], flipped[WEIGHT])
-    weight_below = jnp.where(low, flipped[WEIGHT], crossed[WEIGHT])
+    weight_above = jnp.where(low, middle[AFTER + WEIGHT], middle[WEIGHT])
+    weight_below = jnp.where(low, middle[WEIGHT], middle[AFTER + WEIGHT])
 
     def total(n):
-        return half[LATE + n] + other[LATE + n]
+        return half[LATE + n] + (other[LATE] if n == FLOW_TOP else middle[2 * AFTER - 2 + n])
 
     thermal = half[MAP_THERMAL] + other[MAP_THERMAL]
     height = half[MAP_HEIGHT] + other[MAP_HEIGHT]
@@ -237,13 +237,13 @@
     height_one = height + total(STEP_ONE) + stretch_top * thermal
 
     def above(f):
-        value = jnp.where(low, crossed[f], flipped[f])
+        value = jnp.where(low, middle[AFTER + f], middle[f])
         if f == 0:
-            value = value + jnp.where(lev == 1, flipped[2 * AFTER] * thermal, 0.0)
+            value = value + jnp.where(lev == 1, middle[UPPER] * thermal, 0.0)
         return value + weight_above * height if f == 2 else value
 
     def below(f):
-        value = jnp.where(low, flipped[f], crossed[f])
+        value = jnp.where(low, middle[f], middle[AFTER + f])
         return value + weight_below * height if f == 2 else value
 
     for f, top, bottom in step(
@@ -315,7 +315,6 @@
     tiles = lax.axis_size("tile")
     flip = [(l, l ^ 1) for l in range(groups)]
     inward = [(l, l - 2) for l in range(2, groups, 2)] + [(l, l + 2) for l in range(1, groups - 2, 2)]
-    outward = [(destination, source) for source, destination in inward]
     pair = [(l, l ^ 2) for l in range(groups)]
     mirror = [(l, groups - 2 - (l & ~1) + (l & 1)) for l in range(groups)]
     west = [(t, (t - 1) % tiles) for t in range(tiles)]
@@ -350,10 +349,10 @@
         scratch=[pltpu.VMEM((2 * PIECES * rows, 2 * cols), jnp.float32)],
     )
     sums = sums + lax.ppermute(sums, "lev", pair)
-    own, packed, column = call(
+    own, to_flip, to_other, column = call(
         step_one_kernel,
         (state, flow, mix, stretch, weight, spread, halo, arrived),
-        [state.shape, (MIDDLE, *field), (1, *field)],
+        [state.shape, (AFTER, *field), (AFTER - 1, *field), (1, *field)],
         at={
             7: (
                 (4, cols),
@@ -363,20 +362,20 @@
     )
     half = jnp.concatenate([sums, column, early])
     half = half + lax.ppermute(half, "lev", mirror)
-    flipped = lax.ppermute(packed, "lev", flip)
-    other = lax.ppermute(half, "lev", flip)
+    relayed = lax.ppermute(to_other, "lev", inward)
+    other = lax.ppermute(half[:SOON], "lev", flip)
+    middle = lax.ppermute(jnp.concatenate([to_flip, relayed, half[SOON:]]), "lev", flip)
     (edge,) = call(
         edge_kernel, (own, half, other, flow, mix, spread, weight),
         [(8, cols)], smem=(turned,),
     )
     edge = lax.ppermute(edge, "tile", west)
-    crossed = lax.ppermute(flipped[AFTER : 2 * AFTER], "lev", outward)
     column = half[STEP_TWO:LATE] + other[STEP_TWO:LATE]
     column_other = lax.ppermute(column, "lev", pair)
     out_state, out_height = call(
         step_two_kernel,
         (own, half, other, column, column_other, flow, mix, spread, weight,
-         flipped, crossed, halo, edge),
+         middle, halo, edge),
         [state.shape, field],
     )
     return (out_state[:, :, None], out_height[None])

time: 63.8 us -> 61.3 us (0.961)
  the two profiles are of different devices: /device:TPU:57 before, /device:TPU:61 now
where the time goes in v5:
time: 61.3 us; the launch traced here: 61 us
  starting transfers between devices  34.9 us (57%)
  waiting for transfers between devices  14.1 us (23%)
  Pallas kernels  10.9 us (18%)
  between operations  0.85 us (1%)
    pallas_call x6, Pallas kernels, call(): pl.pallas_call(body, out_shape=[jax.ShapeDtypeStruct(shape, jnp.float32)...  10.9 us
    all_to_all x1, starting transfers between devices, per_device(): lax.all_to_all(packet, 'tile', split_axis=0, concat_axis=0, tiled=True)  8.88 us
    ppermute x1, waiting for transfers between devices, per_device(): edge = lax.ppermute(edge, 'tile', west)  6.53 us
    ppermute x2, starting transfers between devices, per_device(): relayed = lax.ppermute(to_other, 'lev', inward)  5.27 us
    ppermute x1, starting transfers between devices, per_device(): edge = lax.ppermute(edge, 'tile', west)  4.91 us
    ppermute x1, starting transfers between devices, per_device(): halo = lax.ppermute(jnp.concatenate([to_flip, relayed]), 'lev', flip)  4.3 us
    ppermute x1, starting transfers between devices, per_device(): column_other = lax.ppermute(column, 'lev', pair)  4.07 us
    ppermute x2, waiting for transfers between devices, per_device(): relayed = lax.ppermute(to_other, 'lev', inward)  3.33 us
  transfers between devices with their start and end apart: 11, of which 5 were waited for; matrix products, arithmetic and copies ran while one was open for 0% of the time, Pallas kernels for 10%

profile of v5, /device:TPU:61, one launch (start us, length us, event | category | flops | bytes accessed | tf_op | source)
XLA Modules:
  0.0 61.0 jit_solution(9020960127341046151)
XLA Ops:
  0.6 2.6 %shard_map.159 = f32[32,4,640]{2,1,0:T(4,128)} custom-call(s32[32]{0:T(128)} %refs_0_.3, s32[32]{0:T(128)} %bitcast.46, f32[4,2,32,128]{3,2,1,0:T(8,128)} %bitcast.18, f32[2,32,128]{2,1,0:T(8,128)} %bitcast.21, f32[32,512]{1,0:T(8,128)} %bitcast.42, f32[32,512]{1,0:T(8,128)} %bitcast.43, s32[32,512]{1,0:T(8,128)} %bitcast.44, s32[32,512]{1,0:T(8,128)} %bitcast.45), custom_call_target="tpu_custom_call" | custom-call | tf_op jit(solution)/shard_map/pallas_call | solution.py:280
  3.3 0.0 copy-start
  3.3 0.0 copy-start.1
  3.3 0.0 copy-start.2
  3.3 0.0 copy-start.3
  3.3 0.0 copy-start.4
  3.3 8.9 %all-to-all-start = ((f32[32,4,640]{2,1,0:T(4,128)}), f32[32,4,640]{2,1,0:T(4,128)S(1)}, u32[]{:S(2)}, u32[]{:S(2)}) async-start(f32[32,4,640]{2,1,0:T(4,128)} %shard_map.159), calls=%async_computation | async-start | bytes 655360 | tf_op jit(solution)/shard_map/all_to_all | solution.py:337
  12.3 0.5 shard_map.158
  12.8 2.2 %collective-permute-start = (f32[5,32,128]{2,1,0:T(8,128)S(1)}, f32[5,32,128]{2,1,0:T(8,128)S(1)}, u32[]{:S(2)}, u32[]{:S(2)}) collective-permute-start(f32[5,32,128]{2,1,0:T(8,128)S(1)} %get-tuple-element.12), channel_id=1, source_target_pairs={{2,0},{4,2},{6,4},{1,3},{3,5},{5,7},{10,8},{12,10},{14,12},{9,11},... | collective-permute-start | bytes 245768 | tf_op jit(solution)/shard_map/ppermute | solution.py:343
  15.0 3.3 %collective-permute-done = f32[5,32,128]{2,1,0:T(8,128)S(1)} collective-permute-done((f32[5,32,128]{2,1,0:T(8,128)S(1)}, f32[5,32,128]{2,1,0:T(8,128)S(1)}, u32[]{:S(2)}, u32[]{:S(2)}) %collective-permute-start) | collective-permute-done | bytes 81952 | tf_op jit(solution)/shard_map/ppermute | solution.py:343
  18.3 4.3 %collective-permute-start.1 = (f32[10,32,128]{2,1,0:T(8,128)S(1)}, f32[10,32,128]{2,1,0:T(8,128)S(1)}, u32[]{:S(2)}, u32[]{:S(2)}) collective-permute-start(f32[10,32,128]{2,1,0:T(8,128)S(1)} %pad_maximum_fusion.1), channel_id=1, source_target_pairs={{0,1},{1,0},{2,3},{3,2},{4,5},{5,4},{6,7},{7,6},{8,9},{9,8},{10,11... | collective-permute-start | bytes 491528 | tf_op jit(solution)/shard_map/ppermute | solution.py:345
  22.6 0.9 %collective-permute-start.3 = (f32[5,32,128]{2,1,0:T(8,128)S(1)}, f32[5,32,128]{2,1,0:T(8,128)S(1)}, u32[]{:S(2)}, u32[]{:S(2)}) collective-permute-start(f32[5,32,128]{2,1,0:T(8,128)S(1)} %get-tuple-element.15), channel_id=1, source_target_pairs={{0,2},{1,3},{2,0},{3,1},{4,6},{5,7},{6,4},{7,5},{8,10},{9,11},{10,... | collective-permute-start | bytes 245768 | tf_op jit(solution)/shard_map/ppermute | solution.py:344
  23.6 0.0 all-to-all-done.refs_7_.refs_0_
  23.6 3.1 %shard_map.161 = f32[2,32,128]{2,1,0:T(8,128)S(1)} custom-call(f32[32,4,640]{2,1,0:T(4,128)S(1)} %all-to-all-done.refs_7_.refs_0_, f32[32,128]{1,0:T(8,128)S(1)} %bitcast.39, f32[32,128]{1,0:T(8,128)S(1)} %bitcast.40, f32[32,128]{1,0:T(8,128)S(1)} %bitcast.41), custom_call_target="tpu_custom_call" | custom-call | tf_op jit(solution)/shard_map/pallas_call | solution.py:280
  26.7 0.0 copy-start.5
  26.7 0.6 %collective-permute-start.2 = (f32[2,32,128]{2,1,0:T(8,128)S(1)}, f32[2,32,128]{2,1,0:T(8,128)S(1)}, u32[]{:S(2)}, u32[]{:S(2)}) collective-permute-start(f32[2,32,128]{2,1,0:T(8,128)S(1)} %shard_map.161), channel_id=1, source_target_pairs={{0,2},{1,3},{2,0},{3,1},{4,6},{5,7},{6,4},{7,5},{8,10},{9,11},{10,... | collective-permute-start | bytes 98312 | tf_op jit(solution)/shard_map/ppermute | solution.py:351
  27.4 0.0 collective-permute-done.3
  27.4 2.3 %collective-permute-done.1.refs_6_.refs_10_ = f32[10,32,128]{2,1,0:T(8,128)S(1)} collective-permute-done((f32[10,32,128]{2,1,0:T(8,128)S(1)}, f32[10,32,128]{2,1,0:T(8,128)S(1)}, u32[]{:S(2)}, u32[]{:S(2)}) %collective-permute-start.1) | collective-permute-done | bytes 163872 | tf_op jit(solution)/shard_map/ppermute | solution.py:345
  29.7 1.0 %shard_map.160 = (f32[4,2,32,128]{3,2,1,0:T(8,128)S(1)}, f32[6,32,128]{2,1,0:T(8,128)S(1)}, f32[5,32,128]{2,1,0:T(8,128)S(1)}, f32[1,32,128]{2,1,0:T(8,128)S(1)}) custom-call(f32[4,2,32,128]{3,2,1,0:T(8,128)S(1)} %bitcast.20, f32[2,32,128]{2,1,0:T(8,128)S(1)} %bitcast.23, f32[2,32,128]{2,1,0:T(8,128)S(1)} %bitcast.29, f32[4,2,32,128]{3,2,1,0:T(8,128)S(1)} %bitcast.27, ...), custom_call_target="tpu_custom_call" | custom-call | tf_op jit(solution)/shard_map/pallas_call | solution.py:280
  30.8 0.3 collective-permute-start.4
  31.1 3.1 %collective-permute-start.7 = (f32[5,32,128]{2,1,0:T(8,128)S(1)}, f32[5,32,128]{2,1,0:T(8,128)S(1)}, u32[]{:S(2)}, u32[]{:S(2)}) collective-permute-start(f32[5,32,128]{2,1,0:T(8,128)S(1)} %get-tuple-element.17), channel_id=1, source_target_pairs={{2,0},{4,2},{6,4},{1,3},{3,5},{5,7},{10,8},{12,10},{14,12},{9,11},... | collective-permute-start | bytes 245768 | tf_op jit(solution)/shard_map/ppermute | solution.py:365
  34.2 0.4 collective-permute-done.4
  34.7 2.4 %collective-permute-start.5 = (f32[4,32,128]{2,1,0:T(8,128)S(1)}, f32[4,32,128]{2,1,0:T(8,128)S(1)}, u32[]{:S(2)}, u32[]{:S(2)}) collective-permute-start(f32[4,32,128]{2,1,0:T(8,128)S(1)} %get-tuple-element.23), channel_id=1, source_target_pairs={{0,1},{1,0},{2,3},{3,2},{4,5},{5,4},{6,7},{7,6},{8,9},{9,8},{10,11... | collective-permute-start | bytes 196616 | tf_op jit(solution)/shard_map/ppermute | solution.py:366
  37.1 0.0 collective-permute-done.7
  37.2 3.1 %collective-permute-start.8 = (f32[15,32,128]{2,1,0:T(8,128)S(1)}, f32[15,32,128]{2,1,0:T(8,128)S(1)}, u32[]{:S(2)}, u32[]{:S(2)}) collective-permute-start(f32[15,32,128]{2,1,0:T(8,128)S(1)} %pad_maximum_fusion), channel_id=1, source_target_pairs={{0,1},{1,0},{2,3},{3,2},{4,5},{5,4},{6,7},{7,6},{8,9},{9,8},{10,11... | collective-permute-start | bytes 737288 | tf_op jit(solution)/shard_map/ppermute | solution.py:367
  40.3 1.5 %collective-permute-done.5.refs_3_.refs_2_ = f32[4,32,128]{2,1,0:T(8,128)S(1)} collective-permute-done((f32[4,32,128]{2,1,0:T(8,128)S(1)}, f32[4,32,128]{2,1,0:T(8,128)S(1)}, u32[]{:S(2)}, u32[]{:S(2)}) %collective-permute-start.5) | collective-permute-done | bytes 65568 | tf_op jit(solution)/shard_map/ppermute | solution.py:366
  41.8 4.1 %collective-permute-start.6 = (f32[1,32,128]{2,1,0:T(8,128)S(1)}, f32[1,32,128]{2,1,0:T(8,128)S(1)}, u32[]{:S(2)}, u32[]{:S(2)}) collective-permute-start(f32[1,32,128]{2,1,0:T(8,128)S(1)} %slice_add_fusion.refs_3_), channel_id=1, source_target_pairs={{0,2},{1,3},{2,0},{3,1},{4,6},{5,7},{6,4},{7,5},{8,10},{9,11},{10,... | collective-permute-start | bytes 49160 | tf_op jit(solution)/shard_map/ppermute | solution.py:374
  45.9 1.3 %shard_map.162 = f32[8,128]{1,0:T(8,128)S(1)} custom-call(s32[32]{0:T(128)S(1)} %copy-done.9, f32[4,2,32,128]{3,2,1,0:T(8,128)S(1)} %get-tuple-element.13.refs_1_.refs_0_, f32[8,32,128]{2,1,0:T(8,128)S(1)} %fusion.refs_2_.refs_1_, f32[4,32,128]{2,1,0:T(8,128)S(1)} %collective-permute-done.5.refs_3_.refs_2_, f32[2,32,128]{2,1,0:T(8,128)S(1)} %bitcast.24, ...), custom_call_target="tpu_custom_call" | custom-call | tf_op jit(solution)/shard_map/pallas_call | solution.py:280
  47.3 4.9 %collective-permute-start.9 = (f32[8,128]{1,0:T(8,128)S(1)}, f32[8,128]{1,0:T(8,128)S(1)}, u32[]{:S(2)}, u32[]{:S(2)}) collective-permute-start(f32[8,128]{1,0:T(8,128)S(1)} %shard_map.162), channel_id=1, source_target_pairs={{0,248},{8,0},{16,8},{24,16},{32,24},{40,32},{48,40},{56,48},{64,5... | collective-permute-start | bytes 12296 | tf_op jit(solution)/shard_map/ppermute | solution.py:372
  52.2 6.5 %collective-permute-done.9.refs_11_ = f32[8,128]{1,0:T(8,128)S(1)} collective-permute-done((f32[8,128]{1,0:T(8,128)S(1)}, f32[8,128]{1,0:T(8,128)S(1)}, u32[]{:S(2)}, u32[]{:S(2)}) %collective-permute-start.9) | collective-permute-done | bytes 4128 | tf_op jit(solution)/shard_map/ppermute | solution.py:372
  58.7 0.0 collective-permute-done.8.refs_9_
  58.7 2.3 %shard_map.163 = (f32[4,2,32,128]{3,2,1,0:T(8,128)}, f32[32,128]{1,0:T(8,128)}) custom-call(f32[4,2,32,128]{3,2,1,0:T(8,128)S(1)} %get-tuple-element.13.refs_1_.refs_0_, f32[8,32,128]{2,1,0:T(8,128)S(1)} %fusion.refs_2_.refs_1_, f32[4,32,128]{2,1,0:T(8,128)S(1)} %collective-permute-done.5.refs_3_.refs_2_, f32[1,32,128]{2,1,0:T(8,128)S(1)} %slice_add_fusion.refs_3_, ...), custom_call_target="tpu_custom_call" | custom-call | tf_op jit(solution)/shard_map/pallas_call | solution.py:280
  (24 shorter events, 0.1 us)
Async XLA Ops:
  3.3 9.0 %copy-start = (f32[4,2,1,32,128]{4,3,2,1,0:T(8,128)S(1)}, f32[4,2,1,32,128]{4,3,2,1,0:T(8,128)}, u32[]{:S(2)}) copy-start(f32[4,2,1,32,128]{4,3,2,1,0:T(8,128)} %param.15) | copy-start | bytes 393220
  3.3 9.0 %copy-start.1 = (f32[2,1,32,128]{3,2,1,0:T(8,128)S(1)}, f32[2,1,32,128]{3,2,1,0:T(8,128)}, u32[]{:S(2)}) copy-start(f32[2,1,32,128]{3,2,1,0:T(8,128)} %param.17) | copy-start | bytes 98308
  3.3 9.0 %copy-start.2 = (f32[4,2,1,32,128]{4,3,2,1,0:T(8,128)S(1)}, f32[4,2,1,32,128]{4,3,2,1,0:T(8,128)}, u32[]{:S(2)}) copy-start(f32[4,2,1,32,128]{4,3,2,1,0:T(8,128)} %param.20) | copy-start | bytes 393220
  3.3 8.9 %copy-start.3 = (f32[2,1,32,128]{3,2,1,0:T(8,128)S(1)}, f32[2,1,32,128]{3,2,1,0:T(8,128)}, u32[]{:S(2)}) copy-start(f32[2,1,32,128]{3,2,1,0:T(8,128)} %param.19) | copy-start | bytes 98308
  3.3 8.9 %copy-start.4 = (f32[2,1,32,128]{3,2,1,0:T(8,128)S(1)}, f32[2,1,32,128]{3,2,1,0:T(8,128)}, u32[]{:S(2)}) copy-start(f32[2,1,32,128]{3,2,1,0:T(8,128)} %param.21) | copy-start | bytes 98308
  3.3 20.2 %all-to-all-start = ((f32[32,4,640]{2,1,0:T(4,128)}), f32[32,4,640]{2,1,0:T(4,128)S(1)}, u32[]{:S(2)}, u32[]{:S(2)}) async-start(f32[32,4,640]{2,1,0:T(4,128)} %shard_map.159), calls=%async_computation | async-start | bytes 655360 | tf_op jit(solution)/shard_map/all_to_all | solution.py:337
  12.8 5.5 %collective-permute-start = (f32[5,32,128]{2,1,0:T(8,128)S(1)}, f32[5,32,128]{2,1,0:T(8,128)S(1)}, u32[]{:S(2)}, u32[]{:S(2)}) collective-permute-start(f32[5,32,128]{2,1,0:T(8,128)S(1)} %get-tuple-element.12), channel_id=1, source_target_pairs={{2,0},{4,2},{6,4},{1,3},{3,5},{5,7},{10,8},{12,10},{14,12},{9,11},... | collective-permute-start | bytes 245768 | tf_op jit(solution)/shard_map/ppermute | solution.py:343
  18.3 5.2 %copy-start.6 = (f32[1,32,128]{2,1,0:T(8,128)S(1)}, f32[1,32,128]{2,1,0:T(8,128)}, u32[]{:S(2)}) copy-start(f32[1,32,128]{2,1,0:T(8,128)} %param.23) | copy-start | bytes 49156
  18.3 5.2 %copy-start.7 = (f32[1,32,128]{2,1,0:T(8,128)S(1)}, f32[1,32,128]{2,1,0:T(8,128)}, u32[]{:S(2)}) copy-start(f32[1,32,128]{2,1,0:T(8,128)} %param.24) | copy-start | bytes 49156
  18.3 5.2 %copy-start.8 = (f32[1,32,128]{2,1,0:T(8,128)S(1)}, f32[1,32,128]{2,1,0:T(8,128)}, u32[]{:S(2)}) copy-start(f32[1,32,128]{2,1,0:T(8,128)} %param.16) | copy-start | bytes 49156
  18.3 11.3 %collective-permute-start.1 = (f32[10,32,128]{2,1,0:T(8,128)S(1)}, f32[10,32,128]{2,1,0:T(8,128)S(1)}, u32[]{:S(2)}, u32[]{:S(2)}) collective-permute-start(f32[10,32,128]{2,1,0:T(8,128)S(1)} %pad_maximum_fusion.1), channel_id=1, source_target_pairs={{0,1},{1,0},{2,3},{3,2},{4,5},{5,4},{6,7},{7,6},{8,9},{9,8},{10,11... | collective-permute-start | bytes 491528 | tf_op jit(solution)/shard_map/ppermute | solution.py:345
  22.6 4.7 %collective-permute-start.3 = (f32[5,32,128]{2,1,0:T(8,128)S(1)}, f32[5,32,128]{2,1,0:T(8,128)S(1)}, u32[]{:S(2)}, u32[]{:S(2)}) collective-permute-start(f32[5,32,128]{2,1,0:T(8,128)S(1)} %get-tuple-element.15), channel_id=1, source_target_pairs={{0,2},{1,3},{2,0},{3,1},{4,6},{5,7},{6,4},{7,5},{8,10},{9,11},{10,... | collective-permute-start | bytes 245768 | tf_op jit(solution)/shard_map/ppermute | solution.py:344
  26.7 3.0 %copy-start.5 = (f32[1,32,128]{2,1,0:T(8,128)S(1)}, f32[1,32,128]{2,1,0:T(8,128)}, u32[]{:S(2)}) copy-start(f32[1,32,128]{2,1,0:T(8,128)} %param.18) | copy-start | bytes 49156
  26.7 4.0 %collective-permute-start.2 = (f32[2,32,128]{2,1,0:T(8,128)S(1)}, f32[2,32,128]{2,1,0:T(8,128)S(1)}, u32[]{:S(2)}, u32[]{:S(2)}) collective-permute-start(f32[2,32,128]{2,1,0:T(8,128)S(1)} %shard_map.161), channel_id=1, source_target_pairs={{0,2},{1,3},{2,0},{3,1},{4,6},{5,7},{6,4},{7,5},{8,10},{9,11},{10,... | collective-permute-start | bytes 98312 | tf_op jit(solution)/shard_map/ppermute | solution.py:351
  30.8 3.9 %collective-permute-start.4 = (f32[8,32,128]{2,1,0:T(8,128)S(1)}, f32[8,32,128]{2,1,0:T(8,128)S(1)}, u32[]{:S(2)}, u32[]{:S(2)}) collective-permute-start(f32[8,32,128]{2,1,0:T(8,128)S(1)} %pad_maximum_fusion.2), channel_id=1, source_target_pairs={{0,6},{1,7},{2,4},{3,5},{4,2},{5,3},{6,0},{7,1},{8,14},{9,15},{10,... | collective-permute-start | bytes 393224 | tf_op jit(solution)/shard_map/ppermute | solution.py:364
  31.1 6.0 %collective-permute-start.7 = (f32[5,32,128]{2,1,0:T(8,128)S(1)}, f32[5,32,128]{2,1,0:T(8,128)S(1)}, u32[]{:S(2)}, u32[]{:S(2)}) collective-permute-start(f32[5,32,128]{2,1,0:T(8,128)S(1)} %get-tuple-element.17), channel_id=1, source_target_pairs={{2,0},{4,2},{6,4},{1,3},{3,5},{5,7},{10,8},{12,10},{14,12},{9,11},... | collective-permute-start | bytes 245768 | tf_op jit(solution)/shard_map/ppermute | solution.py:365
  34.7 7.1 %collective-permute-start.5 = (f32[4,32,128]{2,1,0:T(8,128)S(1)}, f32[4,32,128]{2,1,0:T(8,128)S(1)}, u32[]{:S(2)}, u32[]{:S(2)}) collective-permute-start(f32[4,32,128]{2,1,0:T(8,128)S(1)} %get-tuple-element.23), channel_id=1, source_target_pairs={{0,1},{1,0},{2,3},{3,2},{4,5},{5,4},{6,7},{7,6},{8,9},{9,8},{10,11... | collective-permute-start | bytes 196616 | tf_op jit(solution)/shard_map/ppermute | solution.py:366
  37.2 21.5 %collective-permute-start.8 = (f32[15,32,128]{2,1,0:T(8,128)S(1)}, f32[15,32,128]{2,1,0:T(8,128)S(1)}, u32[]{:S(2)}, u32[]{:S(2)}) collective-permute-start(f32[15,32,128]{2,1,0:T(8,128)S(1)} %pad_maximum_fusion), channel_id=1, source_target_pairs={{0,1},{1,0},{2,3},{3,2},{4,5},{5,4},{6,7},{7,6},{8,9},{9,8},{10,11... | collective-permute-start | bytes 737288 | tf_op jit(solution)/shard_map/ppermute | solution.py:367
  41.8 4.1 %copy-start.9 = (s32[32]{0:T(128)S(1)}, s32[32]{0:T(128)}, u32[]{:S(2)}) copy-start(s32[32]{0:T(128)} %refs_0_.3) | copy-start | bytes 388
  41.8 16.9 %collective-permute-start.6 = (f32[1,32,128]{2,1,0:T(8,128)S(1)}, f32[1,32,128]{2,1,0:T(8,128)S(1)}, u32[]{:S(2)}, u32[]{:S(2)}) collective-permute-start(f32[1,32,128]{2,1,0:T(8,128)S(1)} %slice_add_fusion.refs_3_), channel_id=1, source_target_pairs={{0,2},{1,3},{2,0},{3,1},{4,6},{5,7},{6,4},{7,5},{8,10},{9,11},{10,... | collective-permute-start | bytes 49160 | tf_op jit(solution)/shard_map/ppermute | solution.py:374
  47.3 11.4 %collective-permute-start.9 = (f32[8,128]{1,0:T(8,128)S(1)}, f32[8,128]{1,0:T(8,128)S(1)}, u32[]{:S(2)}, u32[]{:S(2)}) collective-permute-start(f32[8,128]{1,0:T(8,128)S(1)} %shard_map.162), channel_id=1, source_target_pairs={{0,248},{8,0},{16,8},{24,16},{32,24},{40,32},{48,40},{56,48},{64,5... | collective-permute-start | bytes 12296 | tf_op jit(solution)/shard_map/ppermute | solution.py:372
